TPU v7x, 32 devices: a whole 2x2x4 slice. The times are simulated.
32 devices in a mesh: step: 8 (over y, x, core), lat: 4 (over z).
Axes of the slice: x: 2, y: 2, z: 4, core: 2. Of those that a mesh axis runs over, the one named last changes fastest.
Arguments:
- state_in: bfloat16 [8, 72, 64, 128], P('step', None, 'lat'), may hold values from -6 to 6
- new_state: bfloat16 [72, 64, 128], P(None, 'lat'), may hold values from -6 to 6
- cot_early: bfloat16 [8, 72, 64, 128], P('step', None, 'lat'), may hold values from -6 to 6
- cot_late: bfloat16 [8, 72, 64, 128], P('step', None, 'lat'), may hold values from -6 to 6
- kernel_first: bfloat16 [9, 72, 192], replicated, may hold values from -0.25 to 0.25
- kernel_mid: bfloat16 [9, 192, 192], replicated, may hold values from -0.15625 to 0.15625
- kernel_last: bfloat16 [9, 72, 192], replicated, may hold values from -0.15625 to 0.15625
Outputs:
- advanced: bfloat16 [8, 72, 64, 128], P('step', None, 'lat')
- state_adjoint: bfloat16 [8, 72, 64, 128], P('step', None, 'lat')
- grad_first: float32 [9, 72, 192], replicated
- grad_mid: float32 [9, 192, 192], replicated
- grad_last: float32 [9, 72, 192], replicated
All inputs are finite; a program needn't handle non-finite values.
Results may differ from a plain program's by a relative error of at most 0.008.
Values may be sent and summed in bfloat16 or wider, within the bound.
A program may use at most 64 MiB of HBM per device.

v0:
```python
import math

import jax
import jax.numpy as jnp
from jax import lax
from jax.sharding import PartitionSpec as P


def padded_2(block, sides, width):
    for axis, dim in sides:
        count = lax.axis_size(axis)
        forward = [(i, i + 1) for i in range(count - 1)]
        backward = [(target, source) for source, target in forward]
        low = lax.ppermute(
            lax.slice_in_dim(block, block.shape[dim] - width, None, axis=dim), axis, forward
        )
        high = lax.ppermute(lax.slice_in_dim(block, 0, width, axis=dim), axis, backward)
        block = jnp.concatenate([low, block, high], axis=dim)
    return block


def shifted(block, axis, distance):
    devices = range(lax.axis_size(axis))
    route = [(i - distance, i) for i in devices if i - distance in devices]
    return lax.ppermute(block, axis, route)


def window_at(padded, dilation, row_tap, col_tap, out_rows, out_cols):
    widened = jnp.pad(padded, ((0, 0), (0, 0), (dilation, dilation)))
    return widened[
        :,
        row_tap * dilation : row_tap * dilation + out_rows,
        col_tap * dilation : col_tap * dilation + out_cols,
    ]


def convolve(padded, kernel, dilation, flipped):
    out_rows = padded.shape[1] - 2 * dilation
    out_cols = padded.shape[2]
    pattern = "oc,crw->orw" if flipped else "co,crw->orw"
    summed = None
    for tap_index in range(9):
        window = window_at(padded, dilation, tap_index // 3, tap_index % 3, out_rows, out_cols)
        product = jnp.einsum(pattern, kernel[tap_index], window, preferred_element_type=jnp.float32)
        summed = product if summed is None else summed + product
    return summed


def convolve_back(padded, kernel, dilation, flipped):
    out_rows = padded.shape[1] - 2 * dilation
    out_cols = padded.shape[2]
    pattern = "oc,orw->crw" if flipped else "co,orw->crw"
    summed = None
    for tap_index in range(9):
        window = window_at(
            padded, dilation, 2 - tap_index // 3, 2 - tap_index % 3, out_rows, out_cols
        )
        product = jnp.einsum(pattern, kernel[tap_index], window, preferred_element_type=jnp.float32)
        summed = product if summed is None else summed + product
    return summed


def kernel_terms(padded_in, grad_out, dilation, flipped):
    out_rows = grad_out.shape[1]
    out_cols = grad_out.shape[2]
    pattern = "crw,orw->oc" if flipped else "crw,orw->co"
    listed = []
    for tap_index in range(9):
        window = window_at(padded_in, dilation, tap_index // 3, tap_index % 3, out_rows, out_cols)
        listed.append(jnp.einsum(pattern, window, grad_out, preferred_element_type=jnp.float32))
    return jnp.stack(listed)


def gelu_slope(preact, cotangent):
    return jax.vjp(jax.nn.gelu, preact)[1](cotangent)[0]


def body(state_in, new_state, cot_early, cot_late, kernel_first, kernel_mid, kernel_last):
    band_rows = state_in.shape[2]
    total_rows = band_rows * lax.axis_size("lat")
    band_index = lax.axis_index("lat")

    def inside(values, margin):
        local_rows = jnp.arange(values.shape[1], dtype=jnp.int32)
        global_row = band_index * band_rows + local_rows - margin
        keep = (global_row >= 0) & (global_row < total_rows)
        return jnp.where(keep[None, :, None], values, jnp.zeros_like(values))

    def advance(state):
        extended = padded_2(state, (("lat", 1),), 7)
        pre_first = convolve(extended, kernel_first, 1, False)
        hid_first = inside(jax.nn.gelu(pre_first).astype(jnp.bfloat16), 6)
        pre_mid = convolve(hid_first, kernel_mid, 2, False)
        hid_mid = inside(jax.nn.gelu(pre_mid).astype(jnp.bfloat16), 4)
        pre_last = convolve(hid_mid, kernel_last, 4, True)
        saved = (
            extended[:, 6 : 6 + band_rows + 2],
            hid_first[:, 4 : 4 + band_rows + 4],
            hid_mid,
            pre_first[:, 6 : 6 + band_rows],
            pre_mid[:, 4 : 4 + band_rows],
        )
        output = (state.astype(jnp.float32) + pre_last).astype(jnp.bfloat16)
        return (output, saved)

    def backward(cot_out, saved):
        in_first, in_mid, in_last, pre_first, pre_mid = saved
        pad_last = padded_2(cot_out, (("lat", 1),), 4)
        back_mid = convolve_back(pad_last, kernel_last, 4, True)
        grads_last = kernel_terms(in_last, cot_out, 4, True)
        delta_mid = gelu_slope(pre_mid, back_mid).astype(jnp.bfloat16)
        pad_mid = padded_2(delta_mid, (("lat", 1),), 2)
        back_first = convolve_back(pad_mid, kernel_mid, 2, False)
        grads_mid = kernel_terms(in_mid, delta_mid, 2, False)
        delta_first = gelu_slope(pre_first, back_first).astype(jnp.bfloat16)
        pad_first = padded_2(delta_first, (("lat", 1),), 1)
        back_state = convolve_back(pad_first, kernel_first, 1, False)
        grads_first = kernel_terms(in_first, delta_first, 1, False)
        adjoint = (cot_out.astype(jnp.float32) + back_state).astype(jnp.bfloat16)
        return (adjoint, (grads_first, grads_mid, grads_last))

    early_out, early_saved = advance(state_in[0])
    passed = shifted(early_out, "step", 1)
    late_in = jnp.where(lax.axis_index("step") == 0, new_state, passed)
    late_out, late_saved = advance(late_in)
    late_adjoint, late_grads = backward(cot_late[0], late_saved)
    returned = shifted(late_adjoint, "step", -1)
    early_cot = (cot_early[0].astype(jnp.float32) + returned.astype(jnp.float32)).astype(
        jnp.bfloat16
    )
    state_adjoint, early_grads = backward(early_cot, early_saved)
    grand_total = lax.psum(
        (
            late_grads[0] + early_grads[0],
            late_grads[1] + early_grads[1],
            late_grads[2] + early_grads[2],
        ),
        ("step", "lat"),
    )
    cell_count = 2.0 * lax.axis_size("step") * total_rows * state_in.shape[3]
    grad_scale = 1.0 / math.sqrt(cell_count)
    return (
        late_out[None],
        state_adjoint[None],
        grand_total[0] * grad_scale,
        grand_total[1] * grad_scale,
        grand_total[2] * grad_scale,
    )


def solution(mesh):
    in_specs = (
        P("step", None, "lat", None),
        P(None, "lat", None),
        P("step", None, "lat", None),
        P("step", None, "lat", None),
        P(),
        P(),
        P(),
    )
    out_specs = (P("step", None, "lat", None), P("step", None, "lat", None), P(), P(), P())
    return jax.shard_map(body, mesh=mesh, in_specs=in_specs, out_specs=out_specs, check_vma=False)
```

profile of v0, /device:TPU:0, one launch (start us, length us, event | category | flops | bytes accessed | tf_op | source)
XLA Modules:
  0.0 348.6 jit_solution(4227039910495838793)
XLA Ops:
  7.2 1.1 copy.110
  8.4 5.0 %collective-permute-start = (bf16[72,7,128]{2,0,1:T(8,128)(2,1)S(1)}, bf16[72,7,128]{2,0,1:T(8,128)(2,1)S(1)}, u32[]{:S(2)}, u32[]{:S(2)}) collective-permute-start(bf16[72,7,128]{2,0,1:T(8,128)(2,1)S(1)} %get-tuple-element.27), channel_id=1, source_target_pairs={{0,1},{1,2},{2,3},{4,5},{5,6},{6,7},{8,9},{9,10},{10,11},{12,13},{... | collective-permute-start | bytes 387080 | tf_op jit(solution)/shard_map/ppermute | solution.py:14
  13.3 1.3 collective-permute-start.1
  14.6 1.0 copy.109
  15.7 4.5 %collective-permute-start.5 = (bf16[72,4,128]{2,0,1:T(8,128)(2,1)S(1)}, bf16[72,4,128]{2,0,1:T(8,128)(2,1)S(1)}, u32[]{:S(2)}, u32[]{:S(2)}) collective-permute-start(bf16[72,4,128]{2,0,1:T(8,128)(2,1)S(1)} %get-tuple-element.24), channel_id=1, source_target_pairs={{0,1},{1,2},{2,3},{4,5},{5,6},{6,7},{8,9},{9,10},{10,11},{12,13},{... | collective-permute-start | bytes 221192 | tf_op jit(solution)/shard_map/ppermute | solution.py:14
  20.3 1.3 collective-permute-start.6
  21.6 1.6 fusion.442
  23.2 3.3 collective-permute-done.6
  26.9 1.7 fusion.338
  28.6 1.6 fusion.340
  30.2 1.6 fusion.342
  31.8 1.6 fusion.344
  38.3 3.8 %fusion.75 = (bf16[192,28,128]{2,0,1:T(8,128)(2,1)S(1)}, f32[192,28,128]{2,0,1:T(8,128)}) fusion(pred[28]{0:T(512)(128)(4,1)S(1)} %compare_and_fusion, bf16[9,72,192]{2,1,0:T(8,128)(2,1)S(1)} %copy-done.8, bf16[72,30,128]{2,0,1:T(8,128)(2,1)S(1)} %pad_maximum_fusion, f32[28,128,192]{1,2,0:T(8,128)S(1)} %fusion.470, f32[28,128,192]{1,2,0:T(8,128)S(1)} %fusion.273, ...), kind=kOutput, calls=%fused_computation.167 | convolution fusion | flops 111476736 | bytes 26739200 | tf_op jit(solution)/shard_map/co,crw->orw/dot_general | solution.py:44
  46.5 3.3 fusion.129
  54.0 1.4 collective-permute-start.2
  55.4 1.5 fusion.305
  57.0 1.6 fusion.346
  58.7 3.5 collective-permute-start.3
  62.2 1.3 collective-permute-start.4
  63.5 1.5 fusion.309
  65.1 1.0 slice.996
  66.1 2.9 collective-permute-done.4
  73.4 1.3 fusion.468
  74.7 12.8 %fusion.74 = (bf16[192,28,128]{2,0,1:T(8,128)(2,1)S(1)}, f32[192,28,128]{2,0,1:T(8,128)}) fusion(pred[28]{0:T(512)(128)(4,1)S(1)} %compare_and_fusion, bf16[9,72,192]{2,1,0:T(8,128)(2,1)} %param.11, bf16[72,30,128]{2,0,1:T(8,128)(2,1)S(1)} %pad_maximum_fusion.1, f32[28,128,192]{1,2,0:T(8,128)S(1)} %fusion.468, f32[28,128,192]{1,2,0:T(8,128)S(1)} %fusion.279, ...), kind=kOutput, calls=%fused_computation.166 | convolution fusion | flops 111476736 | bytes 26738716 | tf_op jit(solution)/shard_map/co,crw->orw/dot_general | solution.py:44
  92.0 2.0 fusion.128
  94.0 6.1 %fusion.43 = bf16[192,16,128]{2,0,1:T(8,128)(2,1)S(1)} fusion(f32[16,128,192]{1,2,0:T(8,128)} %fusion.309, f32[16,128,192]{1,2,0:T(8,128)} %fusion.338, f32[16,128,192]{1,2,0:T(8,128)} %fusion.340, f32[192,16,128]{2,0,1:T(8,128)S(1)} %copy-done.6, f32[192,24,128]{2,0,1:T(8,128)S(1)} %get-tuple-element.36, f32[16,128,192]{1,2,0:T(8,128)} %fusion.342, ...), kind=kOutput, calls=%fused_computation.121 | convolution fusion | flops 67633152 | bytes 15273984 | tf_op jit(solution)/shard_map/oc,orw->crw/dot_general | solution.py:58
  103.6 1.3 collective-permute-start.8
  104.9 4.8 %collective-permute-start.7 = (bf16[192,2,128]{2,0,1:T(8,128)(2,1)S(1)}, bf16[192,2,128]{2,0,1:T(8,128)(2,1)S(1)}, u32[]{:S(2)}, u32[]{:S(2)}) collective-permute-start(bf16[192,2,128]{2,0,1:T(8,128)(2,1)S(1)} %get-tuple-element.20), channel_id=1, source_target_pairs={{0,1},{1,2},{2,3},{4,5},{5,6},{6,7},{8,9},{9,10},{10,11},{12,13},{... | collective-permute-start | bytes 294920 | tf_op jit(solution)/shard_map/ppermute | solution.py:14
  118.7 1.0 select_maximum_fusion.2
  122.7 1.0 copy-done.4
  123.8 1.7 fusion.50
  125.8 1.3 collective-permute-start.10
  127.1 5.0 %collective-permute-start.9 = (bf16[192,1,128]{2,0,1:T(8,128)(2,1)S(1)}, bf16[192,1,128]{2,0,1:T(8,128)(2,1)S(1)}, u32[]{:S(2)}, u32[]{:S(2)}) collective-permute-start(bf16[192,1,128]{2,0,1:T(8,128)(2,1)S(1)} %get-tuple-element.17), channel_id=1, source_target_pairs={{0,1},{1,2},{2,3},{4,5},{5,6},{6,7},{8,9},{9,10},{10,11},{12,13},{... | collective-permute-start | bytes 147464 | tf_op jit(solution)/shard_map/ppermute | solution.py:14
  138.7 1.4 collective-permute-start.11
  140.9 1.4 collective-permute-done.11
  146.1 1.3 collective-permute-start.13
  147.4 4.7 %collective-permute-start.12 = (bf16[72,4,128]{2,0,1:T(8,128)(2,1)S(1)}, bf16[72,4,128]{2,0,1:T(8,128)(2,1)S(1)}, u32[]{:S(2)}, u32[]{:S(2)}) collective-permute-start(bf16[72,4,128]{2,0,1:T(8,128)(2,1)S(1)} %get-tuple-element.22), channel_id=1, source_target_pairs={{0,1},{1,2},{2,3},{4,5},{5,6},{6,7},{8,9},{9,10},{10,11},{12,13},{... | collective-permute-start | bytes 221192 | tf_op jit(solution)/shard_map/ppermute | solution.py:14
  158.3 1.7 fusion.57
  164.6 1.3 collective-permute-start.15
  165.9 5.1 %collective-permute-start.14 = (bf16[192,2,128]{2,0,1:T(8,128)(2,1)S(1)}, bf16[192,2,128]{2,0,1:T(8,128)(2,1)S(1)}, u32[]{:S(2)}, u32[]{:S(2)}) collective-permute-start(bf16[192,2,128]{2,0,1:T(8,128)(2,1)S(1)} %get-tuple-element.16), channel_id=1, source_target_pairs={{0,1},{1,2},{2,3},{4,5},{5,6},{6,7},{8,9},{9,10},{10,11},{12,13},{... | collective-permute-start | bytes 294920 | tf_op jit(solution)/shard_map/ppermute | solution.py:14
  171.5 1.5 add.641
  173.0 1.0 select_maximum_fusion
  177.5 1.7 fusion.64
  182.5 1.3 collective-permute-start.17
  183.8 5.2 %collective-permute-start.16 = (bf16[192,1,128]{2,0,1:T(8,128)(2,1)S(1)}, bf16[192,1,128]{2,0,1:T(8,128)(2,1)S(1)}, u32[]{:S(2)}, u32[]{:S(2)}) collective-permute-start(bf16[192,1,128]{2,0,1:T(8,128)(2,1)S(1)} %get-tuple-element.13), channel_id=1, source_target_pairs={{0,1},{1,2},{2,3},{4,5},{5,6},{6,7},{8,9},{9,10},{10,11},{12,13},{... | collective-permute-start | bytes 147464 | tf_op jit(solution)/shard_map/ppermute | solution.py:14
  195.3 142.1 %all-reduce.19.cloned.1.call-done = (f32[9,72,192]{2,1,0:T(8,128)}, f32[9,192,192]{2,1,0:T(8,128)}, f32[9,72,192]{2,1,0:T(8,128)}) async-done(((f32[9,72,192]{2,1,0:T(8,128)}, f32[9,192,192]{2,1,0:T(8,128)}, f32[9,72,192]{2,1,0:T(8,128)}), (f32[9,72,192]{2,1,0:T(8,128)}, f32[9,192,192]{2,1,0:T(8,128)}, f32[9,72,192]{2,1,0:T(8,128)})) %all-reduce.19.cloned.1.call-update) | async-done | bytes 2322448 | tf_op jit(solution)/shard_map/psum | solution.py:132
  337.4 2.9 broadcast_multiply_fusion
  340.3 1.2 broadcast_multiply_fusion.1
  (246 shorter events, 73.4 us)
Async XLA Ops:
  7.2 14.4 %copy-start = (bf16[1,72,16,128]{3,2,1,0:T(8,128)(2,1)S(1)}, bf16[1,72,16,128]{3,2,1,0:T(8,128)(2,1)}, u32[]{:S(2)}) copy-start(bf16[1,72,16,128]{3,2,1,0:T(8,128)(2,1)} %param.10) | copy-start | bytes 884740
  7.2 14.4 %copy-start.7 = (bf16[9,72,192]{2,1,0:T(8,128)(2,1)S(1)}, bf16[9,72,192]{2,1,0:T(8,128)(2,1)}, u32[]{:S(2)}) copy-start(bf16[9,72,192]{2,1,0:T(8,128)(2,1)} %param.13) | copy-start | bytes 746500
  7.2 330.2 %all-reduce.19.cloned.1.call-start = ((), (), s32[]{:S(2)}) async-start(), calls=%async_computation | async-start | bytes 6193152 | tf_op jit(solution)/shard_map/psum | solution.py:132
  8.4 25.0 %collective-permute-start = (bf16[72,7,128]{2,0,1:T(8,128)(2,1)S(1)}, bf16[72,7,128]{2,0,1:T(8,128)(2,1)S(1)}, u32[]{:S(2)}, u32[]{:S(2)}) collective-permute-start(bf16[72,7,128]{2,0,1:T(8,128)(2,1)S(1)} %get-tuple-element.27), channel_id=1, source_target_pairs={{0,1},{1,2},{2,3},{4,5},{5,6},{6,7},{8,9},{9,10},{10,11},{12,13},{... | collective-permute-start | bytes 387080 | tf_op jit(solution)/shard_map/ppermute | solution.py:14
  13.3 20.0 %collective-permute-start.1 = (bf16[72,7,128]{2,0,1:T(8,128)(2,1)S(1)}, bf16[72,7,128]{2,0,1:T(8,128)(2,1)S(1)}, u32[]{:S(2)}, u32[]{:S(2)}) collective-permute-start(bf16[72,7,128]{2,0,1:T(8,128)(2,1)S(1)} %get-tuple-element.28), channel_id=1, source_target_pairs={{1,0},{2,1},{3,2},{5,4},{6,5},{7,6},{9,8},{10,9},{11,10},{13,12},{... | collective-permute-start | bytes 387080 | tf_op jit(solution)/shard_map/ppermute | solution.py:17
  15.7 7.5 %collective-permute-start.5 = (bf16[72,4,128]{2,0,1:T(8,128)(2,1)S(1)}, bf16[72,4,128]{2,0,1:T(8,128)(2,1)S(1)}, u32[]{:S(2)}, u32[]{:S(2)}) collective-permute-start(bf16[72,4,128]{2,0,1:T(8,128)(2,1)S(1)} %get-tuple-element.24), channel_id=1, source_target_pairs={{0,1},{1,2},{2,3},{4,5},{5,6},{6,7},{8,9},{9,10},{10,11},{12,13},{... | collective-permute-start | bytes 221192 | tf_op jit(solution)/shard_map/ppermute | solution.py:14
  20.3 6.2 %collective-permute-start.6 = (bf16[72,4,128]{2,0,1:T(8,128)(2,1)S(1)}, bf16[72,4,128]{2,0,1:T(8,128)(2,1)S(1)}, u32[]{:S(2)}, u32[]{:S(2)}) collective-permute-start(bf16[72,4,128]{2,0,1:T(8,128)(2,1)S(1)} %get-tuple-element.23), channel_id=1, source_target_pairs={{1,0},{2,1},{3,2},{5,4},{6,5},{7,6},{9,8},{10,9},{11,10},{13,12},{... | collective-permute-start | bytes 221192 | tf_op jit(solution)/shard_map/ppermute | solution.py:17
  23.2 5.4 %copy-start.26 = (bf16[72,4,128]{2,0,1:T(8,128)(2,1)}, bf16[72,4,128]{2,0,1:T(8,128)(2,1)S(1)}, u32[]{:S(2)}) copy-start(bf16[72,4,128]{2,0,1:T(8,128)(2,1)S(1)} %collective-permute-done.5) | copy-start | bytes 221188
  26.5 2.1 copy-start.28
  26.9 30.1 %copy-start.2 = (bf16[72,24,136]{2,0,1:T(8,128)(2,1)}, bf16[72,24,136]{2,0,1:T(8,128)(2,1)S(1)}, u32[]{:S(2)}) copy-start(bf16[72,24,136]{2,0,1:T(8,128)(2,1)S(1)} %select_maximum_fusion.10) | copy-start | bytes 1410052
  31.8 1.7 copy-start.8
  33.4 4.4 %copy-start.15 = (bf16[72,7,128]{2,0,1:T(8,128)(2,1)}, bf16[72,7,128]{2,0,1:T(8,128)(2,1)S(1)}, u32[]{:S(2)}) copy-start(bf16[72,7,128]{2,0,1:T(8,128)(2,1)S(1)} %collective-permute-done) | copy-start | bytes 387076
  33.4 4.4 %copy-start.13 = (bf16[72,7,128]{2,0,1:T(8,128)(2,1)}, bf16[72,7,128]{2,0,1:T(8,128)(2,1)S(1)}, u32[]{:S(2)}) copy-start(bf16[72,7,128]{2,0,1:T(8,128)(2,1)S(1)} %collective-permute-done.1) | copy-start | bytes 387076
  38.3 3.8 %copy-start.1 = (bf16[9,192,192]{2,1,0:T(8,128)(2,1)S(1)}, bf16[9,192,192]{2,1,0:T(8,128)(2,1)}, u32[]{:S(2)}) copy-start(bf16[9,192,192]{2,1,0:T(8,128)(2,1)} %param.12) | copy-start | bytes 1990660
  52.7 1.0 copy-start.11
  53.7 1.7 copy-start.29
  54.0 4.7 %copy-start.24 = (bf16[72,16,128]{2,1,0:T(8,128)(2,1)S(1)}, bf16[72,16,128]{2,1,0:T(8,128)(2,1)}, u32[]{:S(2)}) copy-start(bf16[72,16,128]{2,1,0:T(8,128)(2,1)} %param.8) | copy-start | bytes 884740
  54.0 4.6 %collective-permute-start.2 = (bf16[72,16,128]{2,0,1:T(8,128)(2,1)S(1)}, bf16[72,16,128]{2,0,1:T(8,128)(2,1)S(1)}, u32[]{:S(2)}, u32[]{:S(2)}) collective-permute-start(bf16[72,16,128]{2,0,1:T(8,128)(2,1)S(1)} %fusion.105), channel_id=1, source_target_pairs={{0,4},{4,8},{8,12},{12,16},{16,20},{20,24},{24,28},{1,5},{5,9},{9,... | collective-permute-start | bytes 884744 | tf_op jit(solution)/shard_map/ppermute | solution.py:25
  57.0 6.5 %copy-start.27 = (bf16[72,4,128]{2,0,1:T(8,128)(2,1)S(1)}, bf16[72,4,128]{2,0,1:T(8,128)(2,1)}, u32[]{:S(2)}) copy-start(bf16[72,4,128]{2,0,1:T(8,128)(2,1)} %copy-done.26) | copy-start | bytes 221188
  58.7 7.4 %collective-permute-start.3 = (bf16[72,7,128]{2,0,1:T(8,128)(2,1)S(1)}, bf16[72,7,128]{2,0,1:T(8,128)(2,1)S(1)}, u32[]{:S(2)}, u32[]{:S(2)}) collective-permute-start(bf16[72,7,128]{2,0,1:T(8,128)(2,1)S(1)} %get-tuple-element.25), channel_id=1, source_target_pairs={{0,1},{1,2},{2,3},{4,5},{5,6},{6,7},{8,9},{9,10},{10,11},{12,13},{... | collective-permute-start | bytes 387080 | tf_op jit(solution)/shard_map/ppermute | solution.py:14
  62.2 6.8 %collective-permute-start.4 = (bf16[72,7,128]{2,0,1:T(8,128)(2,1)S(1)}, bf16[72,7,128]{2,0,1:T(8,128)(2,1)S(1)}, u32[]{:S(2)}, u32[]{:S(2)}) collective-permute-start(bf16[72,7,128]{2,0,1:T(8,128)(2,1)S(1)} %get-tuple-element.26), channel_id=1, source_target_pairs={{1,0},{2,1},{3,2},{5,4},{6,5},{7,6},{9,8},{10,9},{11,10},{13,12},{... | collective-permute-start | bytes 387080 | tf_op jit(solution)/shard_map/ppermute | solution.py:17
  66.1 7.3 %copy-start.19 = (bf16[72,7,128]{2,0,1:T(8,128)(2,1)}, bf16[72,7,128]{2,0,1:T(8,128)(2,1)S(1)}, u32[]{:S(2)}) copy-start(bf16[72,7,128]{2,0,1:T(8,128)(2,1)S(1)} %collective-permute-done.3) | copy-start | bytes 387076
  69.1 4.3 %copy-start.17 = (bf16[72,7,128]{2,0,1:T(8,128)(2,1)}, bf16[72,7,128]{2,0,1:T(8,128)(2,1)S(1)}, u32[]{:S(2)}) copy-start(bf16[72,7,128]{2,0,1:T(8,128)(2,1)S(1)} %collective-permute-done.4) | copy-start | bytes 387076
  92.0 2.0 copy-start.6
  103.6 15.1 %collective-permute-start.8 = (bf16[192,2,128]{2,0,1:T(8,128)(2,1)S(1)}, bf16[192,2,128]{2,0,1:T(8,128)(2,1)S(1)}, u32[]{:S(2)}, u32[]{:S(2)}) collective-permute-start(bf16[192,2,128]{2,0,1:T(8,128)(2,1)S(1)} %get-tuple-element.19), channel_id=1, source_target_pairs={{1,0},{2,1},{3,2},{5,4},{6,5},{7,6},{9,8},{10,9},{11,10},{13,12},{... | collective-permute-start | bytes 294920 | tf_op jit(solution)/shard_map/ppermute | solution.py:17
  104.9 13.8 %collective-permute-start.7 = (bf16[192,2,128]{2,0,1:T(8,128)(2,1)S(1)}, bf16[192,2,128]{2,0,1:T(8,128)(2,1)S(1)}, u32[]{:S(2)}, u32[]{:S(2)}) collective-permute-start(bf16[192,2,128]{2,0,1:T(8,128)(2,1)S(1)} %get-tuple-element.20), channel_id=1, source_target_pairs={{0,1},{1,2},{2,3},{4,5},{5,6},{6,7},{8,9},{9,10},{10,11},{12,13},{... | collective-permute-start | bytes 294920 | tf_op jit(solution)/shard_map/ppermute | solution.py:14
  122.0 1.8 copy-start.4
  123.8 1.7 copy-start.9
  125.5 7.0 %copy-start.20 = (bf16[72,7,128]{2,0,1:T(8,128)(2,1)S(1)}, bf16[72,7,128]{2,0,1:T(8,128)(2,1)}, u32[]{:S(2)}) copy-start(bf16[72,7,128]{2,0,1:T(8,128)(2,1)} %copy-done.19) | copy-start | bytes 387076
  125.8 9.1 %collective-permute-start.10 = (bf16[192,1,128]{2,0,1:T(8,128)(2,1)S(1)}, bf16[192,1,128]{2,0,1:T(8,128)(2,1)S(1)}, u32[]{:S(2)}, u32[]{:S(2)}) collective-permute-start(bf16[192,1,128]{2,0,1:T(8,128)(2,1)S(1)} %get-tuple-element.18), channel_id=1, source_target_pairs={{1,0},{2,1},{3,2},{5,4},{6,5},{7,6},{9,8},{10,9},{11,10},{13,12},{... | collective-permute-start | bytes 147464 | tf_op jit(solution)/shard_map/ppermute | solution.py:17
  127.1 7.8 %collective-permute-start.9 = (bf16[192,1,128]{2,0,1:T(8,128)(2,1)S(1)}, bf16[192,1,128]{2,0,1:T(8,128)(2,1)S(1)}, u32[]{:S(2)}, u32[]{:S(2)}) collective-permute-start(bf16[192,1,128]{2,0,1:T(8,128)(2,1)S(1)} %get-tuple-element.17), channel_id=1, source_target_pairs={{0,1},{1,2},{2,3},{4,5},{5,6},{6,7},{8,9},{9,10},{10,11},{12,13},{... | collective-permute-start | bytes 147464 | tf_op jit(solution)/shard_map/ppermute | solution.py:14
  138.3 1.8 copy-start.18
  138.6 3.6 %copy-start.25 = (bf16[1,72,16,128]{3,2,1,0:T(8,128)(2,1)S(1)}, bf16[1,72,16,128]{3,2,1,0:T(8,128)(2,1)}, u32[]{:S(2)}) copy-start(bf16[1,72,16,128]{3,2,1,0:T(8,128)(2,1)} %param.9) | copy-start | bytes 884740
  138.7 3.6 %collective-permute-start.11 = (bf16[72,16,128]{2,0,1:T(8,128)(2,1)S(1)}, bf16[72,16,128]{2,0,1:T(8,128)(2,1)S(1)}, u32[]{:S(2)}, u32[]{:S(2)}) collective-permute-start(bf16[72,16,128]{2,0,1:T(8,128)(2,1)S(1)} %fusion.104), channel_id=1, source_target_pairs={{4,0},{8,4},{12,8},{16,12},{20,16},{24,20},{28,24},{5,1},{9,5},{13... | collective-permute-start | bytes 884744 | tf_op jit(solution)/shard_map/ppermute | solution.py:25
  146.1 7.4 %collective-permute-start.13 = (bf16[72,4,128]{2,0,1:T(8,128)(2,1)S(1)}, bf16[72,4,128]{2,0,1:T(8,128)(2,1)S(1)}, u32[]{:S(2)}, u32[]{:S(2)}) collective-permute-start(bf16[72,4,128]{2,0,1:T(8,128)(2,1)S(1)} %get-tuple-element.21), channel_id=1, source_target_pairs={{1,0},{2,1},{3,2},{5,4},{6,5},{7,6},{9,8},{10,9},{11,10},{13,12},{... | collective-permute-start | bytes 221192 | tf_op jit(solution)/shard_map/ppermute | solution.py:17
  147.4 6.5 %collective-permute-start.12 = (bf16[72,4,128]{2,0,1:T(8,128)(2,1)S(1)}, bf16[72,4,128]{2,0,1:T(8,128)(2,1)S(1)}, u32[]{:S(2)}, u32[]{:S(2)}) collective-permute-start(bf16[72,4,128]{2,0,1:T(8,128)(2,1)S(1)} %get-tuple-element.22), channel_id=1, source_target_pairs={{0,1},{1,2},{2,3},{4,5},{5,6},{6,7},{8,9},{9,10},{10,11},{12,13},{... | collective-permute-start | bytes 221192 | tf_op jit(solution)/shard_map/ppermute | solution.py:14
  156.6 1.7 copy-start.5
  160.0 1.2 copy-start.21
  164.6 8.4 %collective-permute-start.15 = (bf16[192,2,128]{2,0,1:T(8,128)(2,1)S(1)}, bf16[192,2,128]{2,0,1:T(8,128)(2,1)S(1)}, u32[]{:S(2)}, u32[]{:S(2)}) collective-permute-start(bf16[192,2,128]{2,0,1:T(8,128)(2,1)S(1)} %get-tuple-element.15), channel_id=1, source_target_pairs={{1,0},{2,1},{3,2},{5,4},{6,5},{7,6},{9,8},{10,9},{11,10},{13,12},{... | collective-permute-start | bytes 294920 | tf_op jit(solution)/shard_map/ppermute | solution.py:17
  165.9 7.1 %collective-permute-start.14 = (bf16[192,2,128]{2,0,1:T(8,128)(2,1)S(1)}, bf16[192,2,128]{2,0,1:T(8,128)(2,1)S(1)}, u32[]{:S(2)}, u32[]{:S(2)}) collective-permute-start(bf16[192,2,128]{2,0,1:T(8,128)(2,1)S(1)} %get-tuple-element.16), channel_id=1, source_target_pairs={{0,1},{1,2},{2,3},{4,5},{5,6},{6,7},{8,9},{9,10},{10,11},{12,13},{... | collective-permute-start | bytes 294920 | tf_op jit(solution)/shard_map/ppermute | solution.py:14
  175.7 1.8 copy-start.3
  180.1 1.2 copy-start.12
  181.3 7.7 %copy-start.14 = (bf16[72,7,128]{2,0,1:T(8,128)(2,1)S(1)}, bf16[72,7,128]{2,0,1:T(8,128)(2,1)}, u32[]{:S(2)}) copy-start(bf16[72,7,128]{2,0,1:T(8,128)(2,1)} %copy-done.13) | copy-start | bytes 387076
  182.5 8.3 %collective-permute-start.17 = (bf16[192,1,128]{2,0,1:T(8,128)(2,1)S(1)}, bf16[192,1,128]{2,0,1:T(8,128)(2,1)S(1)}, u32[]{:S(2)}, u32[]{:S(2)}) collective-permute-start(bf16[192,1,128]{2,0,1:T(8,128)(2,1)S(1)} %get-tuple-element.14), channel_id=1, source_target_pairs={{1,0},{2,1},{3,2},{5,4},{6,5},{7,6},{9,8},{10,9},{11,10},{13,12},{... | collective-permute-start | bytes 147464 | tf_op jit(solution)/shard_map/ppermute | solution.py:17
  183.8 7.0 %collective-permute-start.16 = (bf16[192,1,128]{2,0,1:T(8,128)(2,1)S(1)}, bf16[192,1,128]{2,0,1:T(8,128)(2,1)S(1)}, u32[]{:S(2)}, u32[]{:S(2)}) collective-permute-start(bf16[192,1,128]{2,0,1:T(8,128)(2,1)S(1)} %get-tuple-element.13), channel_id=1, source_target_pairs={{0,1},{1,2},{2,3},{4,5},{5,6},{6,7},{8,9},{9,10},{10,11},{12,13},{... | collective-permute-start | bytes 147464 | tf_op jit(solution)/shard_map/ppermute | solution.py:14
  190.7 1.0 copy-start.10
  337.4 2.9 copy-start.22
  337.4 2.9 copy-start.23
  (1 other events, 0.9 us)
Sparse Core Ops, SparseCore 0:
  190.9 146.4 all-reduce.18
where the time goes:
time: 355 us; the launch traced here: 349 us
  waiting for transfers between devices  150 us (42%)
  matrix products  110 us (31%)
  starting transfers between devices  51 us (14%)
  between operations  15.7 us (4%)
  other arithmetic  12.5 us (4%)
  local copies, waits for them, and re-layouts  9.15 us (3%)
    psum x1, waiting for transfers between devices, body(): lax.psum((late_grads[0] + early_grads[0], late_grads[1] + early_grads[1],...  142 us
    dot_general x54, matrix products, convolve(): jnp.einsum(pattern, kernel[tap_index], window, preferred_element_type=jnp...  47.8 us
    dot_general x54, matrix products, convolve_back(): jnp.einsum(pattern, kernel[tap_index], window, preferred_element_type=jnp...  39.9 us
    ppermute x8, starting transfers between devices, padded_2(): lax.ppermute(lax.slice_in_dim(block, block.shape[dim] - width, None, axis...  37.7 us
    dot_general x54, matrix products, kernel_terms(): jnp.einsum(pattern, window, grad_out, preferred_element_type=jnp.float32)  22.5 us
    ppermute x8, starting transfers between devices, padded_2(): lax.ppermute(lax.slice_in_dim(block, 0, width, axis=dim), axis, backward)  10.3 us
    unnamed x64, local copies, waits for them, and re-layouts  7.89 us
  transfers between devices with their start and end apart: 19, of which 5 were waited for; matrix products, arithmetic and copies ran while one was open for 11% of the time, Pallas kernels for 0%

commit v1 on v0

v1 whole, which is shorter than its diff:
```python
import functools
import math

import jax
import jax.numpy as jnp
from jax import lax
from jax.experimental import pallas as pl
from jax.experimental.pallas import tpu as pltpu
from jax.sharding import PartitionSpec as P

MESH = pl.DeviceIdType.MESH
BF = jnp.bfloat16
F32 = jnp.float32
HALO = 7
NT = (((1,), (1,)), ((), ()))


def gelu_pair(a):
    k = math.sqrt(2.0 / math.pi)
    sq = a * a
    t = jnp.tanh(k * (a + 0.044715 * (sq * a)))
    half = 0.5 * (1.0 + t)
    slope = half + (0.5 * a) * (1.0 - t * t) * (k * (1.0 + (3.0 * 0.044715) * sq))
    return a * half, slope


def spread(dst, value, lane, width, dilation, sign):
    channels = value.shape[0]
    column = lax.broadcasted_iota(jnp.int32, (channels, width), 1)
    for k in range(value.shape[1] // width):
        piece = value[:, k * width : (k + 1) * width]
        for j in range(3):
            shift = sign * dilation * (j - 1)
            if shift == 0:
                moved = piece
            else:
                moved = pltpu.roll(piece, (-shift) % width, 1)
                good = (column + shift >= 0) & (column + shift < width)
                moved = jnp.where(good, moved, 0.0)
            dst[j * channels : (j + 1) * channels, pl.ds(pl.multiple_of(lane + k * width, width), width)] = (
                moved.astype(BF)
            )


def conv_chunk(weights, src, row, dilation, width, back, first_row=0):
    total = None
    for i in range(3):
        offset = (2 - i if back else i) * dilation + first_row
        lane = pl.multiple_of((row + offset) * width, width)
        part = jnp.dot(weights[i], src[:, pl.ds(lane, 2 * width)], preferred_element_type=F32)
        total = part if total is None else total + part
    return total


def forward_part(rows, width, x, mask, w1, w2, w3, out, v3, h1, h2, s1, s2, h1s, h2s):
    chunk = 2 * width
    channels = x.shape[0]

    def lanes(row):
        return pl.ds(pl.multiple_of(row * width, width), chunk)

    @pl.loop(0, (rows + 14) // 2)
    def _(c):
        spread(v3, x[:, lanes(2 * c)].astype(F32), 2 * c * width, width, 1, 1)

    @pl.loop(0, (rows + 12) // 2)
    def _(c):
        value, slope = gelu_pair(conv_chunk(w1, v3, 2 * c, 1, width, False))
        value = jnp.where(mask[:, lanes(2 * c + 1)] > 0, value, 0.0).astype(BF)
        h1[:, lanes(2 * c)] = value
        s1[:, lanes(2 * c)] = slope
        spread(h1s, value.astype(F32), 2 * c * width, width, 2, 1)

    @pl.loop(0, (rows + 8) // 2)
    def _(c):
        value, slope = gelu_pair(conv_chunk(w2, h1s, 2 * c, 2, width, False))
        value = jnp.where(mask[:, lanes(2 * c + 3)] > 0, value, 0.0).astype(BF)
        h2[:, lanes(2 * c)] = value
        s2[:, lanes(2 * c)] = slope
        spread(h2s, value.astype(F32), 2 * c * width, width, 4, 1)

    @pl.loop(0, rows // 2)
    def _(c):
        total = conv_chunk(w3, h2s, 2 * c, 4, width, False)
        base = x[:, lanes(2 * c + HALO)].astype(F32)
        out[:, lanes(2 * c)] = (base + total).astype(BF)


def backward_part(rows, width, cot, mask, w1b, w2b, w3b, v3, h1, h2, s1, s2, adj, tf, tm, tl, c3, g2s, g1s):
    chunk = 2 * width
    band = rows * width

    def lanes(row):
        return pl.ds(pl.multiple_of(row * width, width), chunk)

    @pl.loop(0, (rows + 14) // 2)
    def _(c):
        spread(c3, cot[:, lanes(2 * c)].astype(F32), 2 * c * width, width, 4, -1)

    @pl.loop(0, (rows + 6) // 2)
    def _(c):
        total = conv_chunk(w3b, c3, 2 * c, 4, width, True)
        delta = s2[:, lanes(2 * c + 1)] * total
        delta = jnp.where(mask[:, lanes(2 * c + 4)] > 0, delta, 0.0).astype(BF)
        spread(g2s, delta.astype(F32), 2 * c * width, width, 2, -1)

    @pl.loop(0, (rows + 2) // 2)
    def _(c):
        total = conv_chunk(w2b, g2s, 2 * c, 2, width, True)
        delta = s1[:, lanes(2 * c + 5)] * total
        delta = jnp.where(mask[:, lanes(2 * c + 6)] > 0, delta, 0.0).astype(BF)
        spread(g1s, delta.astype(F32), 2 * c * width, width, 1, -1)

    @pl.loop(0, rows // 2)
    def _(c):
        total = conv_chunk(w1b, g1s, 2 * c, 1, width, True)
        base = cot[:, lanes(2 * c + HALO)].astype(F32)
        adj[:, lanes(2 * c)] = (base + total).astype(BF)

    hid = h1.shape[0]

    def nt(a, b):
        return lax.dot_general(a, b, NT, preferred_element_type=F32)

    @pl.loop(0, 3)
    def _(i):
        def window(row):
            return pl.ds(pl.multiple_of(row * width, width), band)

        tl[i] = nt(c3[:, window(3 + (2 - i) * 4)], h2[:, 4 * width : 4 * width + band])
        tf[i] = nt(v3[:, window(6 + i)], g1s[hid : 2 * hid, width : width + band])
        for j in range(3):
            tm[i, j] = nt(
                h1[:, 6 * width : 6 * width + band],
                g2s[j * hid : (j + 1) * hid, window(1 + (2 - i) * 2)],
            )


def early_forward_kernel(rows, width, x, mask, w1, w2, w3, out, v3, h1, h2, s1, s2, h1s, h2s):
    forward_part(rows, width, x, mask, w1, w2, w3, out, v3, h1, h2, s1, s2, h1s, h2s)


def late_kernel(
    rows, width, x, cot, mask, w1, w2, w3, w1b, w2b, w3b, out, adj, tf, tm, tl,
    v3, h1, h2, s1, s2, h1s, h2s, c3, g2s, g1s,
):
    forward_part(rows, width, x, mask, w1, w2, w3, out, v3, h1, h2, s1, s2, h1s, h2s)
    backward_part(rows, width, cot, mask, w1b, w2b, w3b, v3, h1, h2, s1, s2, adj, tf, tm, tl, c3, g2s, g1s)


def early_backward_kernel(
    rows, width, cot, mask, w1b, w2b, w3b, v3, h1, h2, s1, s2, adj, tf, tm, tl, c3, g2s, g1s
):
    backward_part(rows, width, cot, mask, w1b, w2b, w3b, v3, h1, h2, s1, s2, adj, tf, tm, tl, c3, g2s, g1s)


def reduce_kernel(pairs, lats, scale, src, out, got_a, part_b, got_b, part_c, got_c, full, send, recv):
    step = lax.axis_index("step")
    lat = lax.axis_index("lat")
    core = lax.rem(step, 2)
    pair = step // 2

    partner = {"step": pair * 2 + (1 - core)}

    def pair_peer(k):
        return {"step": lax.rem(pair + k, pairs) * 2 + core}

    def lat_peer(k):
        return {"lat": lax.rem(lat + k, lats)}

    peers = [partner]
    peers += [pair_peer(k) for k in range(1, pairs)]
    peers += [lat_peer(k) for k in range(1, lats)]
    barrier = pltpu.get_barrier_semaphore()
    for peer in peers:
        pl.semaphore_signal(barrier, inc=1, device_id=peer, device_id_type=MESH)
    pl.semaphore_wait(barrier, len(peers))

    count = [0]

    def copy(source, target, peer):
        slot = count[0]
        count[0] += 1
        made = pltpu.make_async_remote_copy(
            src_ref=source, dst_ref=target, send_sem=send.at[slot], recv_sem=recv.at[slot],
            device_id=peer, device_id_type=MESH,
        )
        made.start()
        return made

    def finish(copies):
        for made in copies:
            made.wait()

    finish([copy(src.at[1 - core], got_a, partner)])
    for b in range(pairs):
        part_b[b] = (src[core, b].astype(F32) + got_a[b].astype(F32)).astype(BF)
    finish([copy(part_b.at[lax.rem(pair + k, pairs)], got_b.at[k - 1], pair_peer(k)) for k in range(1, pairs)])
    for c in range(lats):
        total = src[core, pair, c].astype(F32) + got_a[pair, c].astype(F32)
        for k in range(pairs - 1):
            total = total + got_b[k, c].astype(F32)
        part_c[c] = total.astype(BF)
    finish([copy(part_c.at[lax.rem(lat + k, lats)], got_c.at[k - 1], lat_peer(k)) for k in range(1, lats)])
    total = part_c[lat].astype(F32)
    for k in range(lats - 1):
        total = total + got_c[k].astype(F32)
    full[core, pair, lat] = (total * scale).astype(BF)
    piece = full.at[core, pair, lat]
    finish([copy(piece, piece, lat_peer(k)) for k in range(1, lats)])
    piece = full.at[core, pair]
    finish([copy(piece, piece, pair_peer(k)) for k in range(1, pairs)])
    piece = full.at[core]
    finish([copy(piece, piece, partner)])
    for a in range(2):
        for b in range(pairs):
            out[a, b] = full[a, b].astype(F32)


def all_reduce(values, scale):
    pairs = lax.axis_size("step") // 2
    lats = lax.axis_size("lat")
    pieces = 2 * pairs * lats
    total, width = values.shape
    piece = -(-total // (pieces * 16)) * 16
    src = jnp.pad(values, ((0, piece * pieces - total), (0, 0))).reshape(2, pairs, lats, piece, width)
    copies = 2 + 2 * (pairs - 1) + 2 * (lats - 1)
    vmem = pl.BlockSpec(memory_space=pltpu.VMEM)
    out = pl.pallas_call(
        functools.partial(reduce_kernel, pairs, lats, scale),
        out_shape=jax.ShapeDtypeStruct(src.shape, F32),
        in_specs=[vmem],
        out_specs=vmem,
        scratch_shapes=[
            pltpu.VMEM((pairs, lats, piece, width), BF),
            pltpu.VMEM((pairs, lats, piece, width), BF),
            pltpu.VMEM((max(pairs - 1, 1), lats, piece, width), BF),
            pltpu.VMEM((lats, piece, width), BF),
            pltpu.VMEM((max(lats - 1, 1), piece, width), BF),
            pltpu.VMEM(src.shape, BF),
            pltpu.SemaphoreType.DMA((copies,)),
            pltpu.SemaphoreType.DMA((copies,)),
        ],
        compiler_params=pltpu.CompilerParams(collective_id=0, has_side_effects=True),
        name="kernel_term_sum",
    )(src)
    return out.reshape(pieces * piece, width)[:total]


def body(state_in, new_state, cot_early, cot_late, kernel_first, kernel_mid, kernel_last):
    steps, lats = lax.axis_size("step"), lax.axis_size("lat")
    ch, rows, width = new_state.shape
    hid = kernel_mid.shape[1]
    cp = -(-ch // 16) * 16
    band, edge = rows * width, HALO * width
    lat = lax.axis_index("lat")
    step = lax.axis_index("step")

    grid_first = jnp.pad(kernel_first.reshape(3, 3, ch, hid), ((0, 0), (0, 0), (0, cp - ch), (0, 0)))
    grid_last = jnp.pad(kernel_last.reshape(3, 3, ch, hid), ((0, 0), (0, 0), (0, cp - ch), (0, 0)))
    grid_mid = kernel_mid.reshape(3, 3, hid, hid)
    w1 = grid_first.transpose(0, 3, 1, 2).reshape(3, hid, 3 * cp)
    w2 = grid_mid.transpose(0, 3, 1, 2).reshape(3, hid, 3 * hid)
    w3 = grid_last.transpose(0, 2, 1, 3).reshape(3, cp, 3 * hid)
    w1b = grid_first.transpose(0, 2, 1, 3).reshape(3, cp, 3 * hid)
    w2b = grid_mid.transpose(0, 2, 1, 3).reshape(3, hid, 3 * hid)
    w3b = grid_last.transpose(0, 3, 1, 2).reshape(3, hid, 3 * cp)

    ext_row = lat * rows + jnp.arange(rows + 2 * HALO, dtype=jnp.int32) - HALO
    inside = (ext_row >= 0) & (ext_row < rows * lats)
    mask = jnp.repeat(inside.astype(F32), width)[None]

    packed = jnp.stack([state_in[0], new_state, cot_late[0], cot_early[0]]).reshape(4, ch, band)
    low = lax.ppermute(packed[:, :, band - edge :], "lat", [(i, i + 1) for i in range(lats - 1)])
    high = lax.ppermute(packed[:, :, :edge], "lat", [(i + 1, i) for i in range(lats - 1)])
    wide = jnp.concatenate([low, packed, high], axis=2)
    wide = jnp.pad(wide, ((0, 0), (0, cp - ch), (0, 0)))
    state_w, new_w, late_cot_w, early_cot_w = wide[0], wide[1], wide[2], wide[3]

    def to_step(block, distance):
        def send(part, lat_shift):
            route = []
            for s in range(steps):
                for l in range(lats):
                    if 0 <= s + distance < steps and 0 <= l + lat_shift < lats:
                        route.append((s * lats + l, (s + distance) * lats + l + lat_shift))
            return lax.ppermute(part, ("step", "lat"), route)

        trimmed = block[:ch]
        joined = jnp.concatenate(
            [send(trimmed[:, band - edge :], 1), send(trimmed, 0), send(trimmed[:, :edge], -1)], axis=1
        )
        return jnp.pad(joined, ((0, cp - ch), (0, 0)))

    vmem = pl.BlockSpec(memory_space=pltpu.VMEM)
    shape = jax.ShapeDtypeStruct
    lanes_v, lanes_1, lanes_2 = (rows + 14) * width, (rows + 12) * width, (rows + 8) * width
    saved_shapes = [
        ((3 * cp, lanes_v), BF), ((hid, lanes_1), BF), ((hid, lanes_2), BF),
        ((hid, lanes_1), F32), ((hid, lanes_2), F32),
    ]
    fwd_scratch = [((3 * hid, lanes_1), BF), ((3 * hid, lanes_2), BF)]
    bwd_scratch = [
        ((3 * cp, lanes_v), BF), ((3 * hid, (rows + 6) * width), BF), ((3 * hid, (rows + 2) * width), BF)
    ]
    bwd_outs = [
        ((cp, band), BF), ((3, 3 * cp, hid), F32), ((3, 3, hid, hid), F32), ((3, 3 * cp, hid), F32)
    ]

    def call(kernel, name, ins, outs, scratch):
        return pl.pallas_call(
            functools.partial(kernel, rows, width),
            out_shape=[shape(*o) for o in outs],
            in_specs=[vmem] * len(ins),
            out_specs=[vmem] * len(outs),
            scratch_shapes=[pltpu.VMEM(*s) for s in scratch],
            compiler_params=pltpu.CompilerParams(vmem_limit_bytes=56 * 1024 * 1024),
            name=name,
        )(*ins)

    early_out, *saved = call(
        early_forward_kernel, "early_forward", (state_w, mask, w1, w2, w3),
        [((cp, band), BF)] + saved_shapes, fwd_scratch,
    )
    late_in = jnp.where(step == 0, new_w, to_step(early_out, 1))
    late_out, late_adj, *late_terms = call(
        late_kernel, "late_both", (late_in, late_cot_w, mask, w1, w2, w3, w1b, w2b, w3b),
        [((cp, band), BF)] + bwd_outs, saved_shapes + fwd_scratch + bwd_scratch,
    )
    early_cot = (early_cot_w.astype(F32) + to_step(late_adj, -1).astype(F32)).astype(BF)
    state_adj, *early_terms = call(
        early_backward_kernel, "early_backward", (early_cot, mask, w1b, w2b, w3b, *saved),
        bwd_outs, bwd_scratch,
    )

    first, mid, last = (a + b for a, b in zip(late_terms, early_terms))
    first = first.reshape(9, cp, hid)[:, :ch].reshape(9 * ch, hid)
    last = last.reshape(9, cp, hid)[:, :ch].reshape(9 * ch, hid)
    terms = jnp.concatenate([first, mid.reshape(9 * hid, hid), last]).astype(BF)
    n_terms, lane = terms.shape[0], 128
    left, tail = terms[:, :lane], terms[:, lane:]
    fold = lane // tail.shape[1]
    share = n_terms // fold
    folded = jnp.concatenate([tail[k * share : (k + 1) * share] for k in range(fold)], axis=1)
    scale = 1.0 / math.sqrt(2.0 * steps * rows * lats * width)
    summed = all_reduce(jnp.concatenate([left, folded]), scale)
    folded = summed[n_terms:]
    size = hid - lane
    tail = jnp.concatenate([folded[:, k * size : (k + 1) * size] for k in range(fold)], axis=0)
    summed = jnp.concatenate([summed[:n_terms], tail], axis=1)
    return (
        late_out[:ch].reshape(1, ch, rows, width),
        state_adj[:ch].reshape(1, ch, rows, width),
        summed[: 9 * ch].reshape(9, ch, hid),
        summed[9 * ch : 9 * ch + 9 * hid].reshape(9, hid, hid),
        summed[9 * ch + 9 * hid :].reshape(9, ch, hid),
    )


def solution(mesh):
    banded = P("step", None, "lat", None)
    return jax.shard_map(
        body,
        mesh=mesh,
        in_specs=(banded, P(None, "lat", None), banded, banded, P(), P(), P()),
        out_specs=(banded, banded, P(), P(), P()),
        check_vma=False,
    )
```

time: 355 us -> 208 us (0.59); the launches traced: 349 us -> 208 us
  waiting for transfers between devices: 150 us -> 12.1 us
  Pallas kernels: 0 us -> 118 us
  matrix products: 110 us -> 0 us
  starting transfers between devices: 51 us -> 18.2 us
  local copies, waits for them, and re-layouts: 9.15 us -> 35.6 us
  between operations: 15.7 us -> 0.9 us
  other arithmetic: 12.5 us -> 22.8 us
    psum x1 -> x0, waiting for transfers between devices: 142 us -> none  [body(): lax.psum((late_grads[0] + early_grads[0], late_grads[1] + early_grads[1],...]
    pallas_call x0 -> x4, Pallas kernels: none -> 118 us  [the longest x3 81.4 us: call(): pl.pallas_call(functools.partial(kernel, rows, width), out_shape=[shape(*...]
    dot_general x162 -> x0, matrix products: 110 us -> none  [the longest x54 47.8 us: convolve(): jnp.einsum(pattern, kernel[tap_index], window, preferred_element_type=jnp...]
    ppermute x18 -> x8, starting transfers between devices: 50.9 us -> 18.2 us  [the longest x6 12 us: send(): return lax.ppermute(part, ('step', 'lat'), route)]
    concatenate x8 -> x3, other arithmetic: 4.85 us -> 16.6 us  [the longest x1 14.7 us: body(): summed = all_reduce(jnp.concatenate([left, folded]), scale)]
    reshape x0 -> x8, local copies, waits for them, and re-layouts: none -> 11 us  [the longest x1 2.17 us: body(): w2b = grid_mid.transpose(0, 2, 1, 3).reshape(3, hid, 3 * hid)]
    slice x12 -> x10, local copies, waits for them, and re-layouts: 1.26 us -> 8.66 us  [the longest x2 2.67 us: to_step(): trimmed = block[:ch]]
    ppermute x18 -> x8, waiting for transfers between devices: 7.99 us -> 12.1 us  [the longest x6 6.48 us: send(): return lax.ppermute(part, ('step', 'lat'), route)]
  transfers between devices with their start and end apart: 19 -> 8, of which waited for: 5 -> 3; matrix products, arithmetic and copies ran while one was open for 11% -> 9% of each run, Pallas kernels for 0% -> 0%
where the time goes in v1:
time: 208 us
  Pallas kernels  118 us (57%)
  local copies, waits for them, and re-layouts  35.6 us (17%)
  other arithmetic  22.8 us (11%)
  starting transfers between devices  18.2 us (9%)
  waiting for transfers between devices  12.1 us (6%)
    pallas_call x3, Pallas kernels, call(): pl.pallas_call(functools.partial(kernel, rows, width), out_shape=[shape(*...  81.4 us
    pallas_call x1, Pallas kernels, all_reduce(): pl.pallas_call(functools.partial(reduce_kernel, pairs, lats, scale), out_...  36.6 us
    concatenate x1, other arithmetic, body(): summed = all_reduce(jnp.concatenate([left, folded]), scale)  14.7 us
    ppermute x6, starting transfers between devices, send(): return lax.ppermute(part, ('step', 'lat'), route)  12 us
    unnamed x31, local copies, waits for them, and re-layouts  7.04 us
    ppermute x6, waiting for transfers between devices, send(): return lax.ppermute(part, ('step', 'lat'), route)  6.48 us
    ppermute x1, starting transfers between devices, body(): lax.ppermute(packed[:, :, band - edge:], 'lat', [(i, i + 1) for i in rang...  4.99 us
  transfers between devices with their start and end apart: 8, of which 3 were waited for; matrix products, arithmetic and copies ran while one was open for 9% of the time, Pallas kernels for 0%

profile of v1, /device:TPU:0, one launch (start us, length us, event | category | flops | bytes accessed | tf_op | source)
XLA Modules:
  0.0 207.7 jit_solution(6632583401083873249)
XLA Ops:
  0.6 1.1 stack.12
  1.8 1.1 stack.13
  2.9 1.1 stack.15
  4.3 1.0 copy-done.1
  5.3 5.0 %collective-permute-start = (bf16[4,72,896]{2,1,0:T(8,128)(2,1)S(1)}, bf16[4,72,896]{2,1,0:T(8,128)(2,1)S(1)}, u32[]{:S(2)}, u32[]{:S(2)}) collective-permute-start(bf16[4,72,896]{2,1,0:T(8,128)(2,1)S(1)} %get-tuple-element.41), channel_id=1, source_target_pairs={{0,1},{1,2},{2,3},{4,5},{5,6},{6,7},{8,9},{9,10},{10,11},{12,13},{... | collective-permute-start | bytes 1548296 | tf_op jit(solution)/shard_map/ppermute | solution.py:274
  10.3 1.3 collective-permute-start.1
  11.7 0.6 copy.34
  12.5 1.1 pad_bitcast_fusion
  13.7 0.9 copy.21.w1
  14.6 1.4 copy.22.w2
  16.0 1.8 fusion.27
  18.0 1.1 reshape.91.w3
  19.1 2.2 %collective-permute-done = bf16[4,72,896]{2,1,0:T(8,128)(2,1)S(1)} collective-permute-done((bf16[4,72,896]{2,1,0:T(8,128)(2,1)S(1)}, bf16[4,72,896]{2,1,0:T(8,128)(2,1)S(1)}, u32[]{:S(2)}, u32[]{:S(2)}) %collective-permute-start) | collective-permute-done | bytes 516128 | tf_op jit(solution)/shard_map/ppermute | solution.py:274
  21.3 0.8 copy-done.7
  22.1 3.5 %collective-permute-done.1 = bf16[4,72,896]{2,1,0:T(8,128)(2,1)} collective-permute-done((bf16[4,72,896]{2,1,0:T(8,128)(2,1)S(1)}, bf16[4,72,896]{2,1,0:T(8,128)(2,1)}, u32[]{:S(2)}, u32[]{:S(2)}) %collective-permute-start.1) | collective-permute-done | bytes 516128 | tf_op jit(solution)/shard_map/ppermute | solution.py:275
  25.5 1.7 fusion.4
  27.3 1.1 slice_bitcast_fusion.1
  28.4 22.3 %early_forward.1 = (bf16[80,2048]{1,0:T(8,128)(2,1)}, bf16[240,3840]{1,0:T(8,128)(2,1)}, bf16[192,3584]{1,0:T(8,128)(2,1)}, bf16[192,3072]{1,0:T(8,128)(2,1)}, f32[192,3584]{1,0:T(8,128)}, /*index=5*/f32[192,3072]{1,0:T(8,128)}) custom-call(bf16[80,3840]{1,0:T(8,128)(2,1)} %get-tuple-element.38.x, f32[1,3840]{1,0:T(1,128)} %bitcast.83, ...), custom_call_target="tpu_custom_call" | custom-call | tf_op jit(solution)/shard_map/early_forward/pallas_call | solution.py:311
  50.7 1.7 slice.97
  52.4 2.0 collective-permute-start.3
  54.4 1.6 fusion.29
  56.0 5.2 %collective-permute-start.2 = (bf16[72,896]{1,0:T(8,128)(2,1)}, bf16[72,896]{1,0:T(8,128)(2,1)}, u32[]{:S(2)}, u32[]{:S(2)}) collective-permute-start(bf16[72,896]{1,0:T(8,128)(2,1)} %get-tuple-element.49), channel_id=1, source_target_pairs={{0,5},{1,6},{2,7},{4,9},{5,10},{6,11},{8,13},{9,14},{10,15},{12,17... | collective-permute-start | bytes 387080 | tf_op jit(solution)/shard_map/ppermute | solution.py:287
  61.2 1.3 collective-permute-start.4
  62.6 2.1 %reshape.92.w1b = bf16[3,80,576]{2,1,0:T(8,128)(2,1)} reshape(bf16[3,80,3,192]{3,2,1,0:T(4,128)(2,1)} %get-tuple-element.43) | data formatting | bytes 552960 | tf_op jit(solution)/shard_map/reshape | solution.py:265
  64.7 1.9 copy.27.w3b
  66.6 1.3 copy.23
  67.9 2.2 %copy.26.w2b = bf16[3,192,576]{2,1,0:T(8,128)(2,1)} copy(bf16[3,192,576]{1,2,0:T(8,128)(2,1)} %bitcast.68) | data formatting | bytes 1327104 | tf_op jit(solution)/shard_map/reshape | solution.py:266
  70.1 2.0 fusion.22.x
  72.1 37.1 %late_both.1 = (bf16[80,2048]{1,0:T(8,128)(2,1)}, bf16[80,2048]{1,0:T(8,128)(2,1)}, f32[3,240,192]{2,1,0:T(8,128)}, f32[3,3,192,192]{3,2,1,0:T(8,128)}, f32[3,240,192]{2,1,0:T(8,128)}) custom-call(bf16[80,3840]{1,0:T(8,128)(2,1)} %fusion.22.x, bf16[80,3840]{1,0:T(8,128)(2,1)} %get-tuple-element.37.cot, f32[1,3840]{1,0:T(1,128)} %bitcast.84, ...), custom_call_target="tpu_custom_call" | custom-call | tf_op jit(solution)/shard_map/late_both/pallas_call | solution.py:311
  109.2 1.0 slice.103
  110.1 1.3 collective-permute-start.6
  111.4 1.0 fusion.28
  112.4 0.7 collective-permute-start.5
  113.1 1.5 collective-permute-start.7
  114.6 1.0 slice_bitcast_fusion.5
  115.6 0.8 copy.31
  116.3 6.5 %collective-permute-done.7 = bf16[72,896]{1,0:T(8,128)(2,1)S(1)} collective-permute-done((bf16[72,896]{1,0:T(8,128)(2,1)S(1)}, bf16[72,896]{1,0:T(8,128)(2,1)S(1)}, u32[]{:S(2)}, u32[]{:S(2)}) %collective-permute-start.7) | collective-permute-done | bytes 129056 | tf_op jit(solution)/shard_map/ppermute | solution.py:287
  122.8 1.0 fusion.16.cot
  123.8 22.0 %early_backward.1 = (bf16[80,2048]{1,0:T(8,128)(2,1)}, f32[3,240,192]{2,1,0:T(8,128)}, f32[3,3,192,192]{3,2,1,0:T(8,128)}, f32[3,240,192]{2,1,0:T(8,128)}) custom-call(bf16[80,3840]{1,0:T(8,128)(2,1)} %fusion.16.cot, f32[1,3840]{1,0:T(1,128)} %bitcast.85, bf16[3,80,576]{2,1,0:T(8,128)(2,1)} %reshape.92.w1b, bf16[3,192,576]{2,1,0:T(8,128)(2,1)} %copy.26.w2b, ...), custom_call_target="tpu_custom_call" | custom-call | tf_op jit(solution)/shard_map/early_backward/pallas_call | solution.py:311
  145.8 1.6 add_convert_fusion.1
  148.6 14.7 %fusion.19 = bf16[4536,128]{1,0:T(8,128)(2,1)S(1)} fusion(bf16[648,192]{1,0:T(8,128)(2,1)S(1)} %bitcast.75, bf16[1728,192]{1,0:T(8,128)(2,1)S(1)} %bitcast.69, bf16[648,192]{1,0:T(8,128)(2,1)S(1)} %bitcast.76), kind=kLoop, calls=%fused_computation.26 | loop fusion | flops 12192768 | bytes 2322432 | tf_op jit(solution)/shard_map/concatenate | solution.py:346
  163.3 1.1 pad.27
  164.4 36.6 %kernel_term_sum.1 = f32[2,4,4,144,128]{4,3,2,1,0:T(8,128)} custom-call(bf16[2,4,4,144,128]{4,3,2,1,0:T(8,128)(2,1)} %bitcast.65), custom_call_target="tpu_custom_call" | custom-call | tf_op jit(solution)/shard_map/kernel_term_sum/pallas_call | solution.py:229
  201.1 1.6 slice.125
  203.4 1.2 pad_maximum_fusion.3
  204.8 0.7 copy-done.10
  205.6 0.8 copy.32
  206.4 1.3 slice.128
  (41 shorter events, 3.0 us)
Async XLA Ops:
  0.6 3.3 %copy-start.9 = (bf16[1,72,16,128]{3,2,1,0:T(8,128)(2,1)S(1)}, bf16[1,72,16,128]{3,2,1,0:T(8,128)(2,1)}, u32[]{:S(2)}) copy-start(bf16[1,72,16,128]{3,2,1,0:T(8,128)(2,1)} %param.10) | copy-start | bytes 884740
  4.2 8.1 %copy-start.8 = (bf16[9,72,192]{2,1,0:T(8,128)(2,1)S(1)}, bf16[9,72,192]{2,1,0:T(8,128)(2,1)}, u32[]{:S(2)}) copy-start(bf16[9,72,192]{2,1,0:T(8,128)(2,1)} %param.11) | copy-start | bytes 746500
  4.2 1.0 copy-start.1
  5.3 16.0 %collective-permute-start = (bf16[4,72,896]{2,1,0:T(8,128)(2,1)S(1)}, bf16[4,72,896]{2,1,0:T(8,128)(2,1)S(1)}, u32[]{:S(2)}, u32[]{:S(2)}) collective-permute-start(bf16[4,72,896]{2,1,0:T(8,128)(2,1)S(1)} %get-tuple-element.41), channel_id=1, source_target_pairs={{0,1},{1,2},{2,3},{4,5},{5,6},{6,7},{8,9},{9,10},{10,11},{12,13},{... | collective-permute-start | bytes 1548296 | tf_op jit(solution)/shard_map/ppermute | solution.py:274
  10.3 15.2 %collective-permute-start.1 = (bf16[4,72,896]{2,1,0:T(8,128)(2,1)S(1)}, bf16[4,72,896]{2,1,0:T(8,128)(2,1)}, u32[]{:S(2)}, u32[]{:S(2)}) collective-permute-start(bf16[4,72,896]{2,1,0:T(8,128)(2,1)S(1)} %get-tuple-element.42), channel_id=1, source_target_pairs={{1,0},{2,1},{3,2},{5,4},{6,5},{7,6},{9,8},{10,9},{11,10},{13,12},{... | collective-permute-start | bytes 1548296 | tf_op jit(solution)/shard_map/ppermute | solution.py:275
  12.3 2.3 %copy-start.2 = (bf16[9,192,192]{2,1,0:T(8,128)(2,1)S(1)}, bf16[9,192,192]{2,1,0:T(8,128)(2,1)}, u32[]{:S(2)}) copy-start(bf16[9,192,192]{2,1,0:T(8,128)(2,1)} %param.12) | copy-start | bytes 1990660
  21.3 0.8 copy-start.7
  52.4 17.7 %collective-permute-start.3 = (bf16[72,2048]{1,0:T(8,128)(2,1)}, bf16[72,2048]{1,0:T(8,128)(2,1)}, u32[]{:S(2)}, u32[]{:S(2)}) collective-permute-start(bf16[72,2048]{1,0:T(8,128)(2,1)} %slice.97), channel_id=1, source_target_pairs={{0,4},{1,5},{2,6},{3,7},{4,8},{5,9},{6,10},{7,11},{8,12},{9,13},{1... | collective-permute-start | bytes 884744 | tf_op jit(solution)/shard_map/ppermute | solution.py:287
  56.0 14.0 %collective-permute-start.2 = (bf16[72,896]{1,0:T(8,128)(2,1)}, bf16[72,896]{1,0:T(8,128)(2,1)}, u32[]{:S(2)}, u32[]{:S(2)}) collective-permute-start(bf16[72,896]{1,0:T(8,128)(2,1)} %get-tuple-element.49), channel_id=1, source_target_pairs={{0,5},{1,6},{2,7},{4,9},{5,10},{6,11},{8,13},{9,14},{10,15},{12,17... | collective-permute-start | bytes 387080 | tf_op jit(solution)/shard_map/ppermute | solution.py:287
  61.2 8.8 %collective-permute-start.4 = (bf16[72,896]{1,0:T(8,128)(2,1)S(1)}, bf16[72,896]{1,0:T(8,128)(2,1)}, u32[]{:S(2)}, u32[]{:S(2)}) collective-permute-start(bf16[72,896]{1,0:T(8,128)(2,1)S(1)} %get-tuple-element.50), channel_id=1, source_target_pairs={{1,4},{2,5},{3,6},{5,8},{6,9},{7,10},{9,12},{10,13},{11,14},{13,16... | collective-permute-start | bytes 387080 | tf_op jit(solution)/shard_map/ppermute | solution.py:287
  110.1 12.7 %collective-permute-start.6 = (bf16[72,2048]{1,0:T(8,128)(2,1)S(1)}, bf16[72,2048]{1,0:T(8,128)(2,1)S(1)}, u32[]{:S(2)}, u32[]{:S(2)}) collective-permute-start(bf16[72,2048]{1,0:T(8,128)(2,1)S(1)} %slice.103), channel_id=1, source_target_pairs={{4,0},{5,1},{6,2},{7,3},{8,4},{9,5},{10,6},{11,7},{12,8},{13,9},{1... | collective-permute-start | bytes 884744 | tf_op jit(solution)/shard_map/ppermute | solution.py:287
  112.4 3.9 %collective-permute-start.5 = (bf16[72,896]{1,0:T(8,128)(2,1)S(1)}, bf16[72,896]{1,0:T(8,128)(2,1)S(1)}, u32[]{:S(2)}, u32[]{:S(2)}) collective-permute-start(bf16[72,896]{1,0:T(8,128)(2,1)S(1)} %get-tuple-element.47), channel_id=1, source_target_pairs={{4,1},{5,2},{6,3},{8,5},{9,6},{10,7},{12,9},{13,10},{14,11},{16,13... | collective-permute-start | bytes 387080 | tf_op jit(solution)/shard_map/ppermute | solution.py:287
  113.1 9.7 %collective-permute-start.7 = (bf16[72,896]{1,0:T(8,128)(2,1)S(1)}, bf16[72,896]{1,0:T(8,128)(2,1)S(1)}, u32[]{:S(2)}, u32[]{:S(2)}) collective-permute-start(bf16[72,896]{1,0:T(8,128)(2,1)S(1)} %get-tuple-element.48), channel_id=1, source_target_pairs={{5,0},{6,1},{7,2},{9,4},{10,5},{11,6},{13,8},{14,9},{15,10},{17,12... | collective-permute-start | bytes 387080 | tf_op jit(solution)/shard_map/ppermute | solution.py:287
  123.8 22.0 %copy-start.5 = (f32[3,240,192]{2,1,0:T(8,128)S(1)}, f32[3,240,192]{2,1,0:T(8,128)}, u32[]{:S(2)}) copy-start(f32[3,240,192]{2,1,0:T(8,128)} %get-tuple-element.29) | copy-start | bytes 1658884
  123.8 22.0 %copy-start.6 = (f32[3,240,192]{2,1,0:T(8,128)S(1)}, f32[3,240,192]{2,1,0:T(8,128)}, u32[]{:S(2)}) copy-start(f32[3,240,192]{2,1,0:T(8,128)} %get-tuple-element.33) | copy-start | bytes 1658884
  145.8 1.9 copy-start.3
  145.8 2.4 %copy-start.4 = (f32[3,3,192,192]{3,2,1,0:T(8,128)S(1)}, f32[3,3,192,192]{3,2,1,0:T(8,128)}, u32[]{:S(2)}) copy-start(f32[3,3,192,192]{3,2,1,0:T(8,128)} %get-tuple-element.32) | copy-start | bytes 3981316
  201.0 2.1 %copy-start = (f32[2,4,4,144,128]{4,3,2,1,0:T(8,128)S(1)}, f32[2,4,4,144,128]{4,3,2,1,0:T(8,128)}, u32[]{:S(2)}) copy-start(f32[2,4,4,144,128]{4,3,2,1,0:T(8,128)} %kernel_term_sum.1) | copy-start | bytes 7077892
  204.6 1.0 copy-start.10

commit v2 on v1

--- a/solution.py
+++ b/solution.py
@@ -43,13 +43,12 @@
 
 
 def conv_chunk(weights, src, row, dilation, width, back, first_row=0):
-    total = None
+    windows = []
     for i in range(3):
         offset = (2 - i if back else i) * dilation + first_row
         lane = pl.multiple_of((row + offset) * width, width)
-        part = jnp.dot(weights[i], src[:, pl.ds(lane, 2 * width)], preferred_element_type=F32)
-        total = part if total is None else total + part
-    return total
+        windows.append(src[:, pl.ds(lane, 2 * width)])
+    return jnp.dot(weights[...], jnp.concatenate(windows, axis=0), preferred_element_type=F32)
 
 
 def forward_part(rows, width, x, mask, w1, w2, w3, out, v3, h1, h2, s1, s2, h1s, h2s):
@@ -154,11 +153,120 @@
     backward_part(rows, width, cot, mask, w1b, w2b, w3b, v3, h1, h2, s1, s2, adj, tf, tm, tl, c3, g2s, g1s)
 
 
-def reduce_kernel(pairs, lats, scale, src, out, got_a, part_b, got_b, part_c, got_c, full, send, recv):
+def greet(peers):
+    barrier = pltpu.get_barrier_semaphore()
+    total = jnp.int32(0)
+    for present, peer in peers:
+        @pl.when(present)
+        def _(peer=peer):
+            pl.semaphore_signal(barrier, inc=1, device_id=peer, device_id_type=MESH)
+
+        total = total + present.astype(jnp.int32)
+    pl.semaphore_wait(barrier, total)
+
+
+def halo_kernel(rows, width, lats, state, new, late, early, state_w, new_w, late_w, early_w, low, high, send, recv):
+    lat = lax.axis_index("lat")
+    step = lax.axis_index("step")
+    band, edge = rows * width, HALO * width
+    ch = state.shape[0]
+    has_low, has_high = lat > 0, lat < lats - 1
+    greet([(has_low, {"lat": lat - 1}), (has_high, {"lat": lat + 1})])
+    blocks = ((state, state_w), (new, new_w), (late, late_w), (early, early_w))
+
+    def guarded(n, present):
+        return (present & (step == 0)) if n == 1 else present
+
+    ups, downs = [], []
+    for n, (block, wide) in enumerate(blocks):
+        ups.append(pltpu.make_async_remote_copy(
+            src_ref=block.at[:, band - edge :], dst_ref=low.at[n], send_sem=send.at[2 * n], recv_sem=recv.at[2 * n],
+            device_id={"lat": lat + 1}, device_id_type=MESH,
+        ))
+        downs.append(pltpu.make_async_remote_copy(
+            src_ref=block.at[:, :edge], dst_ref=high.at[n], send_sem=send.at[2 * n + 1],
+            recv_sem=recv.at[2 * n + 1], device_id={"lat": lat - 1}, device_id_type=MESH,
+        ))
+        pl.when(guarded(n, has_high))(ups[n].start)
+        pl.when(guarded(n, has_low))(downs[n].start)
+    for n, (block, wide) in enumerate(blocks):
+        wide[:ch, edge : edge + band] = block[...]
+        wide[:ch, :edge] = jnp.zeros((ch, edge), BF)
+        wide[:ch, edge + band :] = jnp.zeros((ch, edge), BF)
+        wide[ch:, :] = jnp.zeros((wide.shape[0] - ch, band + 2 * edge), BF)
+    for n, (block, wide) in enumerate(blocks):
+        @pl.when(guarded(n, has_low))
+        def _(n=n, wide=wide):
+            ups[n].wait_recv()
+            wide[:ch, :edge] = low[n]
+
+        @pl.when(guarded(n, has_high))
+        def _(n=n, wide=wide):
+            downs[n].wait_recv()
+            wide[:ch, edge + band :] = high[n]
+
+        pl.when(guarded(n, has_high))(ups[n].wait_send)
+        pl.when(guarded(n, has_low))(downs[n].wait_send)
+
+
+def step_kernel(rows, width, steps, lats, distance, adds, block, base, out, got, send, recv):
+    lat = lax.axis_index("lat")
+    step = lax.axis_index("step")
+    band, edge = rows * width, HALO * width
+
+    def present(s, l):
+        return (s >= 0) & (s < steps) & (l >= 0) & (l < lats)
+
+    peers = []
+    for s in (step - 1, step + 1):
+        for l in (lat - 1, lat, lat + 1):
+            peers.append((present(s, l), {"step": s, "lat": l}))
+    greet(peers)
+    moves = []
+    for n, (shift, source, target) in enumerate((
+        (1, pl.ds(band - edge, edge), pl.ds(0, edge)),
+        (0, pl.ds(0, band), pl.ds(edge, band)),
+        (-1, pl.ds(0, edge), pl.ds(edge + band, edge)),
+    )):
+        copy = pltpu.make_async_remote_copy(
+            src_ref=block.at[:, source], dst_ref=got.at[:, target], send_sem=send.at[n], recv_sem=recv.at[n],
+            device_id={"step": step + distance, "lat": lat + shift}, device_id_type=MESH,
+        )
+        pl.when(present(step + distance, lat + shift))(copy.start)
+        moves.append((shift, target, copy))
+    for shift, target, copy in moves:
+        arrives = present(step - distance, lat - shift)
+
+        @pl.when(arrives)
+        def _(target=target, copy=copy):
+            copy.wait_recv()
+            if adds:
+                out[:, target] = (base[:, target].astype(F32) + got[:, target].astype(F32)).astype(BF)
+            else:
+                out[:, target] = got[:, target]
+
+        @pl.when(jnp.logical_not(arrives))
+        def _(target=target):
+            if adds:
+                out[:, target] = base[:, target]
+            else:
+                first = (step == 0).astype(F32)
+                out[:, target] = (base[:, target].astype(F32) * first).astype(BF)
+
+        pl.when(present(step + distance, lat + shift))(copy.wait_send)
+
+
+def reduce_kernel(
+    pairs, lats, piece, scale, *refs
+):
+    terms, outs = refs[:6], refs[6:9]
+    src, got_a, part_b, got_b, part_c, got_c, full, send, recv = refs[9:]
+    late_first, late_mid, late_last, early_first, early_mid, early_last = terms
     step = lax.axis_index("step")
     lat = lax.axis_index("lat")
     core = lax.rem(step, 2)
     pair = step // 2
+    half, wedge = pairs * lats * piece, lats * piece
 
     partner = {"step": pair * 2 + (1 - core)}
 
@@ -174,9 +282,36 @@
     barrier = pltpu.get_barrier_semaphore()
     for peer in peers:
         pl.semaphore_signal(barrier, inc=1, device_id=peer, device_id_type=MESH)
+
+    cp, hid = late_first.shape[1], late_mid.shape[1]
+    lane = src.shape[1]
+    rest = hid - lane
+    tap_rows = 3 * cp + hid + hid // 2
+    taps = late_first.shape[0]
+
+    @pl.loop(0, taps)
+    def _(t):
+        start = pl.multiple_of(t * tap_rows, 16)
+        first = late_first[t] + early_first[t]
+        last = late_last[t] + early_last[t]
+        mid = late_mid[t] + early_mid[t]
+        src[pl.ds(start, cp), :] = first[:, :lane].astype(BF)
+        src[pl.ds(start + cp, cp), :] = last[:, :lane].astype(BF)
+        src[pl.ds(start + 2 * cp, cp), :] = jnp.concatenate([first[:, lane:], last[:, lane:]], axis=1).astype(BF)
+        src[pl.ds(start + 3 * cp, hid), :] = mid[:, :lane].astype(BF)
+        src[pl.ds(start + 3 * cp + hid, hid // 2), :] = jnp.concatenate(
+            [mid[: hid // 2, lane:], mid[hid // 2 :, lane:]], axis=1
+        ).astype(BF)
+
+    used = taps * tap_rows
+    if used < src.shape[0]:
+        src[used:, :] = jnp.zeros((src.shape[0] - used, lane), BF)
     pl.semaphore_wait(barrier, len(peers))
 
     count = [0]
+
+    def rows_at(start, size):
+        return pl.ds(pl.multiple_of(start, 16), size)
 
     def copy(source, target, peer):
         slot = count[0]
@@ -192,59 +327,86 @@
         for made in copies:
             made.wait()
 
-    finish([copy(src.at[1 - core], got_a, partner)])
+    finish([copy(src.at[rows_at((1 - core) * half, half)], got_a, partner)])
     for b in range(pairs):
-        part_b[b] = (src[core, b].astype(F32) + got_a[b].astype(F32)).astype(BF)
-    finish([copy(part_b.at[lax.rem(pair + k, pairs)], got_b.at[k - 1], pair_peer(k)) for k in range(1, pairs)])
+        mine = src[rows_at(core * half + b * wedge, wedge), :].astype(F32)
+        part_b[b * wedge : (b + 1) * wedge, :] = (mine + got_a[b * wedge : (b + 1) * wedge, :].astype(F32)).astype(BF)
+    finish([
+        copy(part_b.at[rows_at(lax.rem(pair + k, pairs) * wedge, wedge)], got_b.at[k - 1], pair_peer(k))
+        for k in range(1, pairs)
+    ])
     for c in range(lats):
-        total = src[core, pair, c].astype(F32) + got_a[pair, c].astype(F32)
+        total = src[rows_at(core * half + pair * wedge + c * piece, piece), :].astype(F32)
+        total = total + got_a[rows_at(pair * wedge + c * piece, piece), :].astype(F32)
         for k in range(pairs - 1):
-            total = total + got_b[k, c].astype(F32)
-        part_c[c] = total.astype(BF)
-    finish([copy(part_c.at[lax.rem(lat + k, lats)], got_c.at[k - 1], lat_peer(k)) for k in range(1, lats)])
-    total = part_c[lat].astype(F32)
+            total = total + got_b[k, c * piece : (c + 1) * piece, :].astype(F32)
+        part_c[c * piece : (c + 1) * piece, :] = total.astype(BF)
+    finish([
+        copy(part_c.at[rows_at(lax.rem(lat + k, lats) * piece, piece)], got_c.at[k - 1], lat_peer(k))
+        for k in range(1, lats)
+    ])
+    total = part_c[rows_at(lat * piece, piece), :].astype(F32)
     for k in range(lats - 1):
         total = total + got_c[k].astype(F32)
-    full[core, pair, lat] = (total * scale).astype(BF)
-    piece = full.at[core, pair, lat]
-    finish([copy(piece, piece, lat_peer(k)) for k in range(1, lats)])
-    piece = full.at[core, pair]
-    finish([copy(piece, piece, pair_peer(k)) for k in range(1, pairs)])
-    piece = full.at[core]
-    finish([copy(piece, piece, partner)])
-    for a in range(2):
-        for b in range(pairs):
-            out[a, b] = full[a, b].astype(F32)
-
-
-def all_reduce(values, scale):
+    mine = core * half + pair * wedge + lat * piece
+    full[rows_at(mine, piece), :] = (total * scale).astype(BF)
+    held = full.at[rows_at(mine, piece)]
+    finish([copy(held, held, lat_peer(k)) for k in range(1, lats)])
+    held = full.at[rows_at(core * half + pair * wedge, wedge)]
+    finish([copy(held, held, pair_peer(k)) for k in range(1, pairs)])
+    held = full.at[rows_at(core * half, half)]
+    finish([copy(held, held, partner)])
+
+    out_first, out_mid, out_last = outs
+    ch = out_first.shape[1]
+
+    @pl.loop(0, taps)
+    def _(t):
+        start = pl.multiple_of(t * tap_rows, 16)
+        tails = full[pl.ds(start + 2 * cp, cp), :].astype(F32)
+        out_first[t, :, :lane] = full[pl.ds(start, cp), :].astype(F32)[:ch]
+        out_first[t, :, lane:] = tails[:ch, :rest]
+        out_last[t, :, :lane] = full[pl.ds(start + cp, cp), :].astype(F32)[:ch]
+        out_last[t, :, lane:] = tails[:ch, rest:]
+        tails = full[pl.ds(start + 3 * cp + hid, hid // 2), :].astype(F32)
+        out_mid[t, :, :lane] = full[pl.ds(start + 3 * cp, hid), :].astype(F32)
+        out_mid[t, : hid // 2, lane:] = tails[:, :rest]
+        out_mid[t, hid // 2 :, lane:] = tails[:, rest:]
+
+
+def all_reduce(late_terms, early_terms, ch, scale):
     pairs = lax.axis_size("step") // 2
     lats = lax.axis_size("lat")
     pieces = 2 * pairs * lats
-    total, width = values.shape
+    taps, cp, hid = late_terms[0].shape
+    lane = 128
+    total = taps * (3 * cp + hid + hid // 2)
     piece = -(-total // (pieces * 16)) * 16
-    src = jnp.pad(values, ((0, piece * pieces - total), (0, 0))).reshape(2, pairs, lats, piece, width)
     copies = 2 + 2 * (pairs - 1) + 2 * (lats - 1)
     vmem = pl.BlockSpec(memory_space=pltpu.VMEM)
-    out = pl.pallas_call(
-        functools.partial(reduce_kernel, pairs, lats, scale),
-        out_shape=jax.ShapeDtypeStruct(src.shape, F32),
-        in_specs=[vmem],
-        out_specs=vmem,
+    return pl.pallas_call(
+        functools.partial(reduce_kernel, pairs, lats, piece, scale),
+        out_shape=[
+            jax.ShapeDtypeStruct((taps, ch, hid), F32),
+            jax.ShapeDtypeStruct((taps, hid, hid), F32),
+            jax.ShapeDtypeStruct((taps, ch, hid), F32),
+        ],
+        in_specs=[vmem] * 6,
+        out_specs=[vmem] * 3,
         scratch_shapes=[
-            pltpu.VMEM((pairs, lats, piece, width), BF),
-            pltpu.VMEM((pairs, lats, piece, width), BF),
-            pltpu.VMEM((max(pairs - 1, 1), lats, piece, width), BF),
-            pltpu.VMEM((lats, piece, width), BF),
-            pltpu.VMEM((max(lats - 1, 1), piece, width), BF),
-            pltpu.VMEM(src.shape, BF),
+            pltpu.VMEM((pieces * piece, lane), BF),
+            pltpu.VMEM((pairs * lats * piece, lane), BF),
+            pltpu.VMEM((pairs * lats * piece, lane), BF),
+            pltpu.VMEM((max(pairs - 1, 1), lats * piece, lane), BF),
+            pltpu.VMEM((lats * piece, lane), BF),
+            pltpu.VMEM((max(lats - 1, 1), piece, lane), BF),
+            pltpu.VMEM((pieces * piece, lane), BF),
             pltpu.SemaphoreType.DMA((copies,)),
             pltpu.SemaphoreType.DMA((copies,)),
         ],
         compiler_params=pltpu.CompilerParams(collective_id=0, has_side_effects=True),
         name="kernel_term_sum",
-    )(src)
-    return out.reshape(pieces * piece, width)[:total]
+    )(*late_terms, *early_terms)
 
 
 def body(state_in, new_state, cot_early, cot_late, kernel_first, kernel_mid, kernel_last):
@@ -254,43 +416,49 @@
     cp = -(-ch // 16) * 16
     band, edge = rows * width, HALO * width
     lat = lax.axis_index("lat")
-    step = lax.axis_index("step")
 
     grid_first = jnp.pad(kernel_first.reshape(3, 3, ch, hid), ((0, 0), (0, 0), (0, cp - ch), (0, 0)))
     grid_last = jnp.pad(kernel_last.reshape(3, 3, ch, hid), ((0, 0), (0, 0), (0, cp - ch), (0, 0)))
     grid_mid = kernel_mid.reshape(3, 3, hid, hid)
-    w1 = grid_first.transpose(0, 3, 1, 2).reshape(3, hid, 3 * cp)
-    w2 = grid_mid.transpose(0, 3, 1, 2).reshape(3, hid, 3 * hid)
-    w3 = grid_last.transpose(0, 2, 1, 3).reshape(3, cp, 3 * hid)
-    w1b = grid_first.transpose(0, 2, 1, 3).reshape(3, cp, 3 * hid)
-    w2b = grid_mid.transpose(0, 2, 1, 3).reshape(3, hid, 3 * hid)
-    w3b = grid_last.transpose(0, 3, 1, 2).reshape(3, hid, 3 * cp)
+    w1 = grid_first.transpose(3, 0, 1, 2).reshape(hid, 9 * cp)
+    w2 = grid_mid.transpose(3, 0, 1, 2).reshape(hid, 9 * hid)
+    w3 = grid_last.transpose(2, 0, 1, 3).reshape(cp, 9 * hid)
+    w1b = grid_first.transpose(2, 0, 1, 3).reshape(cp, 9 * hid)
+    w2b = grid_mid.transpose(2, 0, 1, 3).reshape(hid, 9 * hid)
+    w3b = grid_last.transpose(3, 0, 1, 2).reshape(hid, 9 * cp)
 
     ext_row = lat * rows + jnp.arange(rows + 2 * HALO, dtype=jnp.int32) - HALO
     inside = (ext_row >= 0) & (ext_row < rows * lats)
     mask = jnp.repeat(inside.astype(F32), width)[None]
 
-    packed = jnp.stack([state_in[0], new_state, cot_late[0], cot_early[0]]).reshape(4, ch, band)
-    low = lax.ppermute(packed[:, :, band - edge :], "lat", [(i, i + 1) for i in range(lats - 1)])
-    high = lax.ppermute(packed[:, :, :edge], "lat", [(i + 1, i) for i in range(lats - 1)])
-    wide = jnp.concatenate([low, packed, high], axis=2)
-    wide = jnp.pad(wide, ((0, 0), (0, cp - ch), (0, 0)))
-    state_w, new_w, late_cot_w, early_cot_w = wide[0], wide[1], wide[2], wide[3]
-
-    def to_step(block, distance):
-        def send(part, lat_shift):
-            route = []
-            for s in range(steps):
-                for l in range(lats):
-                    if 0 <= s + distance < steps and 0 <= l + lat_shift < lats:
-                        route.append((s * lats + l, (s + distance) * lats + l + lat_shift))
-            return lax.ppermute(part, ("step", "lat"), route)
-
-        trimmed = block[:ch]
-        joined = jnp.concatenate(
-            [send(trimmed[:, band - edge :], 1), send(trimmed, 0), send(trimmed[:, :edge], -1)], axis=1
-        )
-        return jnp.pad(joined, ((0, cp - ch), (0, 0)))
+    vmem_spec = pl.BlockSpec(memory_space=pltpu.VMEM)
+    wide_shape = jax.ShapeDtypeStruct((cp, band + 2 * edge), BF)
+    state_w, new_w, late_cot_w, early_cot_w = pl.pallas_call(
+        functools.partial(halo_kernel, rows, width, lats),
+        out_shape=[wide_shape] * 4,
+        in_specs=[vmem_spec] * 4,
+        out_specs=[vmem_spec] * 4,
+        scratch_shapes=[
+            pltpu.VMEM((4, ch, edge), BF), pltpu.VMEM((4, ch, edge), BF),
+            pltpu.SemaphoreType.DMA((8,)), pltpu.SemaphoreType.DMA((8,)),
+        ],
+        compiler_params=pltpu.CompilerParams(collective_id=1, has_side_effects=True),
+        name="halos",
+    )(*(block.reshape(ch, band) for block in (state_in[0], new_state, cot_late[0], cot_early[0])))
+
+    def to_step(block, base, distance, adds):
+        return pl.pallas_call(
+            functools.partial(step_kernel, rows, width, steps, lats, distance, adds),
+            out_shape=wide_shape,
+            in_specs=[vmem_spec] * 2,
+            out_specs=vmem_spec,
+            scratch_shapes=[
+                pltpu.VMEM(wide_shape.shape, BF),
+                pltpu.SemaphoreType.DMA((3,)), pltpu.SemaphoreType.DMA((3,)),
+            ],
+            compiler_params=pltpu.CompilerParams(collective_id=3 if adds else 2, has_side_effects=True),
+            name="step_cotangent" if adds else "step_state",
+        )(block, base)
 
     vmem = pl.BlockSpec(memory_space=pltpu.VMEM)
     shape = jax.ShapeDtypeStruct
@@ -322,38 +490,29 @@
         early_forward_kernel, "early_forward", (state_w, mask, w1, w2, w3),
         [((cp, band), BF)] + saved_shapes, fwd_scratch,
     )
-    late_in = jnp.where(step == 0, new_w, to_step(early_out, 1))
+    late_in = to_step(early_out, new_w, 1, False)
     late_out, late_adj, *late_terms = call(
         late_kernel, "late_both", (late_in, late_cot_w, mask, w1, w2, w3, w1b, w2b, w3b),
         [((cp, band), BF)] + bwd_outs, saved_shapes + fwd_scratch + bwd_scratch,
     )
-    early_cot = (early_cot_w.astype(F32) + to_step(late_adj, -1).astype(F32)).astype(BF)
+    early_cot = to_step(late_adj, early_cot_w, -1, True)
     state_adj, *early_terms = call(
         early_backward_kernel, "early_backward", (early_cot, mask, w1b, w2b, w3b, *saved),
         bwd_outs, bwd_scratch,
     )
 
-    first, mid, last = (a + b for a, b in zip(late_terms, early_terms))
-    first = first.reshape(9, cp, hid)[:, :ch].reshape(9 * ch, hid)
-    last = last.reshape(9, cp, hid)[:, :ch].reshape(9 * ch, hid)
-    terms = jnp.concatenate([first, mid.reshape(9 * hid, hid), last]).astype(BF)
-    n_terms, lane = terms.shape[0], 128
-    left, tail = terms[:, :lane], terms[:, lane:]
-    fold = lane // tail.shape[1]
-    share = n_terms // fold
-    folded = jnp.concatenate([tail[k * share : (k + 1) * share] for k in range(fold)], axis=1)
+    def by_tap(terms):
+        first, mid, last = terms
+        return first.reshape(9, cp, hid), mid.reshape(9, hid, hid), last.reshape(9, cp, hid)
+
     scale = 1.0 / math.sqrt(2.0 * steps * rows * lats * width)
-    summed = all_reduce(jnp.concatenate([left, folded]), scale)
-    folded = summed[n_terms:]
-    size = hid - lane
-    tail = jnp.concatenate([folded[:, k * size : (k + 1) * size] for k in range(fold)], axis=0)
-    summed = jnp.concatenate([summed[:n_terms], tail], axis=1)
+    first, mid, last = all_reduce(by_tap(late_terms), by_tap(early_terms), ch, scale)
     return (
         late_out[:ch].reshape(1, ch, rows, width),
         state_adj[:ch].reshape(1, ch, rows, width),
-        summed[: 9 * ch].reshape(9, ch, hid),
-        summed[9 * ch : 9 * ch + 9 * hid].reshape(9, hid, hid),
-        summed[9 * ch + 9 * hid :].reshape(9, ch, hid),
+        first,
+        mid,
+        last,
     )
 
 

time: 208 us -> 180 us (0.87)
  Pallas kernels: 118 us -> 159 us
  other arithmetic: 22.8 us -> 0.01 us
  starting transfers between devices: 18.2 us -> 0 us
  local copies, waits for them, and re-layouts: 35.6 us -> 20.4 us
  waiting for transfers between devices: 12.1 us -> 0 us
    pallas_call x1 -> x4, Pallas kernels: 36.6 us -> 78 us  [the longest x1 41.3 us: all_reduce(): pl.pallas_call(functools.partial(reduce_kernel, pairs, lats, piece, scale...]
    ppermute x8 -> x0, starting transfers between devices: 18.2 us -> none  [the longest x6 12 us: send(): return lax.ppermute(part, ('step', 'lat'), route)]
    concatenate x3 -> x0, other arithmetic: 16.6 us -> none  [the longest x1 14.7 us: body(): summed = all_reduce(jnp.concatenate([left, folded]), scale)]
    ppermute x8 -> x0, waiting for transfers between devices: 12.1 us -> none  [the longest x6 6.48 us: send(): return lax.ppermute(part, ('step', 'lat'), route)]
    slice x10 -> x0, local copies, waits for them, and re-layouts: 8.66 us -> none  [the longest x2 2.67 us: to_step(): trimmed = block[:ch]]
    unnamed x31 -> x23, local copies, waits for them, and re-layouts: 7.04 us -> 9.89 us
    another operation x5 -> x1, local copies, waits for them, and re-layouts: 3.47 us -> 0.93 us  [body(): block.reshape(ch, band)]
    reshape x6 -> x7, local copies, waits for them, and re-layouts: 9.5 us -> 7.05 us  [the longest x1 1.17 us: body(): w2 = grid_mid.transpose(3, 0, 1, 2).reshape(hid, 9 * hid)]
  transfers between devices with their start and end apart: 8 -> 0, of which waited for: 3 -> 0; matrix products, arithmetic and copies ran while one was open for 9% -> 0% of each run, Pallas kernels for 0% -> 0%
where the time goes in v2:
time: 180 us
  Pallas kernels  159 us (88%)
  local copies, waits for them, and re-layouts  20.4 us (11%)
    pallas_call x3, Pallas kernels, call(): pl.pallas_call(functools.partial(kernel, rows, width), out_shape=[shape(*...  80.6 us
    pallas_call x1, Pallas kernels, all_reduce(): pl.pallas_call(functools.partial(reduce_kernel, pairs, lats, piece, scale...  41.3 us
    pallas_call x2, Pallas kernels, to_step(): pl.pallas_call(functools.partial(step_kernel, rows, width, steps, lats, d...  19.2 us
    pallas_call x1, Pallas kernels, body(): pl.pallas_call(functools.partial(halo_kernel, rows, width, lats), out_sha...  17.6 us
    unnamed x23, local copies, waits for them, and re-layouts  9.89 us

profile of v2, /device:TPU:0, one launch (start us, length us, event | category | flops | bytes accessed | tf_op | source)
XLA Modules:
  0.0 179.8 jit_solution(14481747064398911174)
XLA Ops:
  0.6 0.1 broadcast_bitcast_fusion
  0.7 0.6 copy.42
  1.3 1.1 copy.18
  2.5 0.0 copy-start.3
  2.5 0.0 copy-start.4
  2.5 0.3 pad_bitcast_fusion
  2.8 0.0 copy-start.5
  2.8 0.0 copy-start.6
  2.9 1.0 reshape.71.w1b
  3.9 0.0 copy-start
  3.9 0.1 copy.19
  3.9 0.9 copy.21.w1
  4.8 0.0 copy-done.3
  4.8 0.0 copy-done.4
  4.8 0.0 copy-start.2
  4.8 0.9 copy_bitcast_fusion.2
  5.8 0.0 copy-done.5
  5.8 0.0 copy-done.6
  5.8 0.9 copy_bitcast_fusion
  6.7 0.0 copy-done
  6.7 1.2 copy.22.w2
  7.9 0.0 copy-done.2
  7.9 0.1 fusion
  7.9 0.9 copy.27.w3b
  8.8 0.3 copy.20
  9.0 1.0 reshape.70.w3
  10.1 0.7 copy.23
  10.8 1.2 copy.26.w2b
  12.0 17.6 %halos.1 = (bf16[80,3840]{1,0:T(8,128)(2,1)}, bf16[80,3840]{1,0:T(8,128)(2,1)}, bf16[80,3840]{1,0:T(8,128)(2,1)}, bf16[80,3840]{1,0:T(8,128)(2,1)}) custom-call(bf16[72,2048]{1,0:T(8,128)(2,1)} %get-tuple-element.56.state, bf16[72,2048]{1,0:T(8,128)(2,1)} %get-tuple-element.55.new, bf16[72,2048]{1,0:T(8,128)(2,1)} %get-tuple-element.54.late, ...), custom_call_target="tpu_custom_call" | custom-call | tf_op jit(solution)/shard_map/halos/pallas_call | solution.py:436
  29.5 22.1 %early_forward.1 = (bf16[80,2048]{1,0:T(8,128)(2,1)}, bf16[240,3840]{1,0:T(8,128)(2,1)}, bf16[192,3584]{1,0:T(8,128)(2,1)}, bf16[192,3072]{1,0:T(8,128)(2,1)}, f32[192,3584]{1,0:T(8,128)}, /*index=5*/f32[192,3072]{1,0:T(8,128)}) custom-call(bf16[80,3840]{1,0:T(8,128)(2,1)} %get-tuple-element.27.x, f32[1,3840]{1,0:T(1,128)} %bitcast.74, ...), custom_call_target="tpu_custom_call" | custom-call | tf_op jit(solution)/shard_map/early_forward/pallas_call | solution.py:479
  51.6 5.3 %step_state.1.x = bf16[80,3840]{1,0:T(8,128)(2,1)} custom-call(bf16[80,2048]{1,0:T(8,128)(2,1)} %get-tuple-element.28.block, bf16[80,3840]{1,0:T(8,128)(2,1)} %get-tuple-element.29.base), custom_call_target="tpu_custom_call" | custom-call | tf_op jit(solution)/shard_map/step_state/pallas_call | solution.py:450
  56.9 36.8 %late_both.1 = (bf16[80,2048]{1,0:T(8,128)(2,1)}, bf16[80,2048]{1,0:T(8,128)(2,1)}, f32[3,240,192]{2,1,0:T(8,128)}, f32[3,3,192,192]{3,2,1,0:T(8,128)}, f32[3,240,192]{2,1,0:T(8,128)}) custom-call(bf16[80,3840]{1,0:T(8,128)(2,1)} %step_state.1.x, bf16[80,3840]{1,0:T(8,128)(2,1)} %get-tuple-element.30.cot, f32[1,3840]{1,0:T(1,128)} %bitcast.75, ...), custom_call_target="tpu_custom_call" | custom-call | tf_op jit(solution)/shard_map/late_both/pallas_call | solution.py:479
  93.7 1.0 slice_bitcast_fusion.1
  94.7 0.8 copy.35
  95.5 13.9 %step_cotangent.1.cot = bf16[80,3840]{1,0:T(8,128)(2,1)} custom-call(bf16[80,2048]{1,0:T(8,128)(2,1)} %get-tuple-element.32.block, bf16[80,3840]{1,0:T(8,128)(2,1)} %get-tuple-element.33.base), custom_call_target="tpu_custom_call" | custom-call | tf_op jit(solution)/shard_map/step_cotangent/pallas_call | solution.py:450
  109.4 21.8 %early_backward.1 = (bf16[80,2048]{1,0:T(8,128)(2,1)}, f32[3,240,192]{2,1,0:T(8,128)}, f32[3,3,192,192]{3,2,1,0:T(8,128)}, f32[3,240,192]{2,1,0:T(8,128)}) custom-call(bf16[80,3840]{1,0:T(8,128)(2,1)} %step_cotangent.1.cot, f32[1,3840]{1,0:T(1,128)} %bitcast.76, bf16[80,1728]{1,0:T(8,128)(2,1)} %reshape.71.w1b, bf16[192,1728]{1,0:T(8,128)(2,1)} %copy.26.w2b, ...), custom_call_target="tpu_custom_call" | custom-call | tf_op jit(solution)/shard_map/early_backward/pallas_call | solution.py:479
  131.1 1.0 slice_bitcast_fusion
  132.1 0.8 copy.36
  132.9 41.3 %kernel_term_sum.1 = (f32[9,72,192]{2,1,0:T(8,128)}, f32[9,192,192]{2,1,0:T(8,128)}, f32[9,72,192]{2,1,0:T(8,128)}) custom-call(f32[9,80,192]{2,1,0:T(8,128)} %bitcast.62, f32[9,192,192]{2,1,0:T(8,128)} %bitcast.58, f32[9,80,192]{2,1,0:T(8,128)} %bitcast.63, f32[9,80,192]{2,1,0:T(8,128)} %bitcast.64, f32[9,192,192]{2,1,0:T(8,128)} %bitcast.59, ...), custom_call_target="tpu_custom_call" | custom-call | tf_op jit(solution)/shard_map/kernel_term_sum/pallas_call | solution.py:387
  174.2 2.0 %copy.46 = f32[9,72,192]{2,1,0:T(8,128)} copy(f32[9,72,192]{2,1,0:T(8,128)} %get-tuple-element.64) | data formatting | bytes 995328
  176.1 0.0 copy-start.1
  176.1 2.9 %copy.47 = f32[9,192,192]{2,1,0:T(8,128)} copy(f32[9,192,192]{2,1,0:T(8,128)} %get-tuple-element.65) | data formatting | bytes 2654208
  179.0 0.0 copy-done.1
  179.0 0.8 copy.48
  (1 shorter events, 0.0 us)
Async XLA Ops:
  2.5 2.3 %copy-start.3 = (bf16[72,16,128]{2,1,0:T(8,128)(2,1)S(1)}, bf16[72,16,128]{2,1,0:T(8,128)(2,1)}, u32[]{:S(2)}) copy-start(bf16[72,16,128]{2,1,0:T(8,128)(2,1)} %param.8) | copy-start | bytes 884740
  2.5 2.3 %copy-start.4 = (bf16[1,72,16,128]{3,2,1,0:T(8,128)(2,1)S(1)}, bf16[1,72,16,128]{3,2,1,0:T(8,128)(2,1)}, u32[]{:S(2)}) copy-start(bf16[1,72,16,128]{3,2,1,0:T(8,128)(2,1)} %param.7) | copy-start | bytes 884740
  2.8 2.9 %copy-start.5 = (bf16[1,72,16,128]{3,2,1,0:T(8,128)(2,1)S(1)}, bf16[1,72,16,128]{3,2,1,0:T(8,128)(2,1)}, u32[]{:S(2)}) copy-start(bf16[1,72,16,128]{3,2,1,0:T(8,128)(2,1)} %param.9) | copy-start | bytes 884740
  2.8 2.9 %copy-start.6 = (bf16[1,72,16,128]{3,2,1,0:T(8,128)(2,1)S(1)}, bf16[1,72,16,128]{3,2,1,0:T(8,128)(2,1)}, u32[]{:S(2)}) copy-start(bf16[1,72,16,128]{3,2,1,0:T(8,128)(2,1)} %param.10) | copy-start | bytes 884740
  3.9 2.8 %copy-start = (bf16[9,192,192]{2,1,0:T(8,128)(2,1)S(1)}, bf16[9,192,192]{2,1,0:T(8,128)(2,1)}, u32[]{:S(2)}) copy-start(bf16[9,192,192]{2,1,0:T(8,128)(2,1)} %param.12) | copy-start | bytes 1990660
  4.8 3.0 %copy-start.2 = (bf16[9,72,192]{2,1,0:T(8,128)(2,1)S(1)}, bf16[9,72,192]{2,1,0:T(8,128)(2,1)}, u32[]{:S(2)}) copy-start(bf16[9,72,192]{2,1,0:T(8,128)(2,1)} %param.13) | copy-start | bytes 746500
  176.1 2.9 %copy-start.1 = (f32[9,72,192]{2,1,0:T(8,128)S(1)}, f32[9,72,192]{2,1,0:T(8,128)}, u32[]{:S(2)}) copy-start(f32[9,72,192]{2,1,0:T(8,128)} %get-tuple-element.66) | copy-start | bytes 1492996

commit v3 on v2

--- a/solution.py
+++ b/solution.py
@@ -53,7 +53,7 @@
 
 def forward_part(rows, width, x, mask, w1, w2, w3, out, v3, h1, h2, s1, s2, h1s, h2s):
     chunk = 2 * width
-    channels = x.shape[0]
+    hid = s1.shape[0]
 
     def lanes(row):
         return pl.ds(pl.multiple_of(row * width, width), chunk)
@@ -62,27 +62,28 @@
     def _(c):
         spread(v3, x[:, lanes(2 * c)].astype(F32), 2 * c * width, width, 1, 1)
 
-    @pl.loop(0, (rows + 12) // 2)
+    @pl.loop(0, (rows + 12) // 2, unroll=2)
     def _(c):
         value, slope = gelu_pair(conv_chunk(w1, v3, 2 * c, 1, width, False))
         value = jnp.where(mask[:, lanes(2 * c + 1)] > 0, value, 0.0).astype(BF)
-        h1[:, lanes(2 * c)] = value
-        s1[:, lanes(2 * c)] = slope
+        s1[:, lanes(2 * c)] = slope.astype(BF)
         spread(h1s, value.astype(F32), 2 * c * width, width, 2, 1)
 
-    @pl.loop(0, (rows + 8) // 2)
+    @pl.loop(0, (rows + 8) // 2, unroll=2)
     def _(c):
         value, slope = gelu_pair(conv_chunk(w2, h1s, 2 * c, 2, width, False))
         value = jnp.where(mask[:, lanes(2 * c + 3)] > 0, value, 0.0).astype(BF)
-        h2[:, lanes(2 * c)] = value
-        s2[:, lanes(2 * c)] = slope
+        s2[:, lanes(2 * c)] = slope.astype(BF)
         spread(h2s, value.astype(F32), 2 * c * width, width, 4, 1)
 
-    @pl.loop(0, rows // 2)
+    @pl.loop(0, rows // 2, unroll=2)
     def _(c):
         total = conv_chunk(w3, h2s, 2 * c, 4, width, False)
         base = x[:, lanes(2 * c + HALO)].astype(F32)
         out[:, lanes(2 * c)] = (base + total).astype(BF)
+        if h1 is not None:
+            h1[:, lanes(2 * c)] = h1s[hid : 2 * hid, lanes(2 * c + 6)]
+            h2[:, lanes(2 * c)] = h2s[hid : 2 * hid, lanes(2 * c + 4)]
 
 
 def backward_part(rows, width, cot, mask, w1b, w2b, w3b, v3, h1, h2, s1, s2, adj, tf, tm, tl, c3, g2s, g1s):
@@ -99,18 +100,18 @@
     @pl.loop(0, (rows + 6) // 2)
     def _(c):
         total = conv_chunk(w3b, c3, 2 * c, 4, width, True)
-        delta = s2[:, lanes(2 * c + 1)] * total
+        delta = s2[:, lanes(2 * c + 1)].astype(F32) * total
         delta = jnp.where(mask[:, lanes(2 * c + 4)] > 0, delta, 0.0).astype(BF)
         spread(g2s, delta.astype(F32), 2 * c * width, width, 2, -1)
 
     @pl.loop(0, (rows + 2) // 2)
     def _(c):
         total = conv_chunk(w2b, g2s, 2 * c, 2, width, True)
-        delta = s1[:, lanes(2 * c + 5)] * total
+        delta = s1[:, lanes(2 * c + 5)].astype(F32) * total
         delta = jnp.where(mask[:, lanes(2 * c + 6)] > 0, delta, 0.0).astype(BF)
         spread(g1s, delta.astype(F32), 2 * c * width, width, 1, -1)
 
-    @pl.loop(0, rows // 2)
+    @pl.loop(0, rows // 2, unroll=2)
     def _(c):
         total = conv_chunk(w1b, g1s, 2 * c, 1, width, True)
         base = cot[:, lanes(2 * c + HALO)].astype(F32)
@@ -126,11 +127,11 @@
         def window(row):
             return pl.ds(pl.multiple_of(row * width, width), band)
 
-        tl[i] = nt(c3[:, window(3 + (2 - i) * 4)], h2[:, 4 * width : 4 * width + band])
+        tl[i] = nt(c3[:, window(3 + (2 - i) * 4)], h2[...])
         tf[i] = nt(v3[:, window(6 + i)], g1s[hid : 2 * hid, width : width + band])
         for j in range(3):
             tm[i, j] = nt(
-                h1[:, 6 * width : 6 * width + band],
+                h1[...],
                 g2s[j * hid : (j + 1) * hid, window(1 + (2 - i) * 2)],
             )
 
@@ -141,9 +142,12 @@
 
 def late_kernel(
     rows, width, x, cot, mask, w1, w2, w3, w1b, w2b, w3b, out, adj, tf, tm, tl,
-    v3, h1, h2, s1, s2, h1s, h2s, c3, g2s, g1s,
+    v3, s1, s2, h1s, h2s, c3, g2s, g1s,
 ):
-    forward_part(rows, width, x, mask, w1, w2, w3, out, v3, h1, h2, s1, s2, h1s, h2s)
+    forward_part(rows, width, x, mask, w1, w2, w3, out, v3, None, None, s1, s2, h1s, h2s)
+    hid, band = s1.shape[0], rows * width
+    h1 = h1s.at[hid : 2 * hid, 6 * width : 6 * width + band]
+    h2 = h2s.at[hid : 2 * hid, 4 * width : 4 * width + band]
     backward_part(rows, width, cot, mask, w1b, w2b, w3b, v3, h1, h2, s1, s2, adj, tf, tm, tl, c3, g2s, g1s)
 
 
@@ -259,14 +263,15 @@
 def reduce_kernel(
     pairs, lats, piece, scale, *refs
 ):
-    terms, outs = refs[:6], refs[6:9]
-    src, got_a, part_b, got_b, part_c, got_c, full, send, recv = refs[9:]
+    terms, out = refs[:6], refs[6]
+    src, got_a, part_b, got_b, part_c, got_c, full, send, recv = refs[7:]
     late_first, late_mid, late_last, early_first, early_mid, early_last = terms
     step = lax.axis_index("step")
     lat = lax.axis_index("lat")
     core = lax.rem(step, 2)
     pair = step // 2
     half, wedge = pairs * lats * piece, lats * piece
+    segments = got_a.shape[0]
 
     partner = {"step": pair * 2 + (1 - core)}
 
@@ -327,51 +332,73 @@
         for made in copies:
             made.wait()
 
-    finish([copy(src.at[rows_at((1 - core) * half, half)], got_a, partner)])
-    for b in range(pairs):
-        mine = src[rows_at(core * half + b * wedge, wedge), :].astype(F32)
-        part_b[b * wedge : (b + 1) * wedge, :] = (mine + got_a[b * wedge : (b + 1) * wedge, :].astype(F32)).astype(BF)
-    finish([
-        copy(part_b.at[rows_at(lax.rem(pair + k, pairs) * wedge, wedge)], got_b.at[k - 1], pair_peer(k))
-        for k in range(1, pairs)
-    ])
-    for c in range(lats):
-        total = src[rows_at(core * half + pair * wedge + c * piece, piece), :].astype(F32)
-        total = total + got_a[rows_at(pair * wedge + c * piece, piece), :].astype(F32)
-        for k in range(pairs - 1):
-            total = total + got_b[k, c * piece : (c + 1) * piece, :].astype(F32)
-        part_c[c * piece : (c + 1) * piece, :] = total.astype(BF)
-    finish([
-        copy(part_c.at[rows_at(lax.rem(lat + k, lats) * piece, piece)], got_c.at[k - 1], lat_peer(k))
-        for k in range(1, lats)
-    ])
-    total = part_c[rows_at(lat * piece, piece), :].astype(F32)
-    for k in range(lats - 1):
-        total = total + got_c[k].astype(F32)
-    mine = core * half + pair * wedge + lat * piece
-    full[rows_at(mine, piece), :] = (total * scale).astype(BF)
-    held = full.at[rows_at(mine, piece)]
-    finish([copy(held, held, lat_peer(k)) for k in range(1, lats)])
-    held = full.at[rows_at(core * half + pair * wedge, wedge)]
-    finish([copy(held, held, pair_peer(k)) for k in range(1, pairs)])
-    held = full.at[rows_at(core * half, half)]
-    finish([copy(held, held, partner)])
-
-    out_first, out_mid, out_last = outs
-    ch = out_first.shape[1]
-
-    @pl.loop(0, taps)
-    def _(t):
-        start = pl.multiple_of(t * tap_rows, 16)
-        tails = full[pl.ds(start + 2 * cp, cp), :].astype(F32)
-        out_first[t, :, :lane] = full[pl.ds(start, cp), :].astype(F32)[:ch]
-        out_first[t, :, lane:] = tails[:ch, :rest]
-        out_last[t, :, :lane] = full[pl.ds(start + cp, cp), :].astype(F32)[:ch]
-        out_last[t, :, lane:] = tails[:ch, rest:]
-        tails = full[pl.ds(start + 3 * cp + hid, hid // 2), :].astype(F32)
-        out_mid[t, :, :lane] = full[pl.ds(start + 3 * cp, hid), :].astype(F32)
-        out_mid[t, : hid // 2, lane:] = tails[:, :rest]
-        out_mid[t, hid // 2 :, lane:] = tails[:, rest:]
+    def stage_b(q):
+        base = q * 2 * half + core * half
+        for b in range(pairs):
+            mine = src[rows_at(base + b * wedge, wedge), :].astype(F32)
+            theirs = got_a[q, b * wedge : (b + 1) * wedge, :].astype(F32)
+            part_b[q, b * wedge : (b + 1) * wedge, :] = (mine + theirs).astype(BF)
+        return [
+            copy(part_b.at[q, rows_at(lax.rem(pair + k, pairs) * wedge, wedge)], got_b.at[q, k - 1], pair_peer(k))
+            for k in range(1, pairs)
+        ]
+
+    def stage_c(q):
+        base = q * 2 * half + core * half + pair * wedge
+        for c in range(lats):
+            total = src[rows_at(base + c * piece, piece), :].astype(F32)
+            total = total + got_a[q, rows_at(pair * wedge + c * piece, piece), :].astype(F32)
+            for k in range(pairs - 1):
+                total = total + got_b[q, k, c * piece : (c + 1) * piece, :].astype(F32)
+            part_c[q, c * piece : (c + 1) * piece, :] = total.astype(BF)
+        return [
+            copy(part_c.at[q, rows_at(lax.rem(lat + k, lats) * piece, piece)], got_c.at[q, k - 1], lat_peer(k))
+            for k in range(1, lats)
+        ]
+
+    def spread_c(q):
+        total = part_c[q, rows_at(lat * piece, piece), :].astype(F32)
+        for k in range(lats - 1):
+            total = total + got_c[q, k].astype(F32)
+        mine = rows_at(q * 2 * half + core * half + pair * wedge + lat * piece, piece)
+        full[mine, :] = (total * scale).astype(BF)
+        return [copy(full.at[mine], full.at[mine], lat_peer(k)) for k in range(1, lats)]
+
+    def spread_b(q):
+        held = full.at[rows_at(q * 2 * half + core * half + pair * wedge, wedge)]
+        return [copy(held, held, pair_peer(k)) for k in range(1, pairs)]
+
+    def spread_a(q):
+        held = full.at[rows_at(q * 2 * half + core * half, half)]
+        return [copy(held, held, partner)]
+
+    flying = [
+        [copy(src.at[rows_at(q * 2 * half + (1 - core) * half, half)], got_a.at[q], partner)]
+        for q in range(segments)
+    ]
+    for stage in (stage_b, stage_c, spread_c, spread_b, spread_a):
+        for q in range(segments):
+            finish(flying[q])
+            flying[q] = stage(q)
+    for q in range(segments):
+        finish(flying[q])
+    out[...] = full[...]
+
+
+def unpack_kernel(packed, out_first, out_mid, out_last):
+    ch, hid = out_first.shape[1:]
+    lane = packed.shape[1]
+    rest = hid - lane
+    cp = (packed.shape[0] - hid - hid // 2) // 3
+    tails = packed[2 * cp : 3 * cp, :].astype(F32)
+    out_first[0, :, :lane] = packed[:cp, :].astype(F32)[:ch]
+    out_first[0, :, lane:] = tails[:ch, :rest]
+    out_last[0, :, :lane] = packed[cp : 2 * cp, :].astype(F32)[:ch]
+    out_last[0, :, lane:] = tails[:ch, rest:]
+    tails = packed[3 * cp + hid :, :].astype(F32)
+    out_mid[0, :, :lane] = packed[3 * cp : 3 * cp + hid, :].astype(F32)
+    out_mid[0, : hid // 2, lane:] = tails[:, :rest]
+    out_mid[0, hid // 2 :, lane:] = tails[:, rest:]
 
 
 def all_reduce(late_terms, early_terms, ch, scale):
@@ -380,33 +407,47 @@
     pieces = 2 * pairs * lats
     taps, cp, hid = late_terms[0].shape
     lane = 128
-    total = taps * (3 * cp + hid + hid // 2)
-    piece = -(-total // (pieces * 16)) * 16
-    copies = 2 + 2 * (pairs - 1) + 2 * (lats - 1)
+    tap_rows = 3 * cp + hid + hid // 2
+    segments = 2
+    piece = -(-taps * tap_rows // (segments * pieces * 16)) * 16
+    rows = segments * pieces * piece
+    copies = segments * (2 + 2 * (pairs - 1) + 2 * (lats - 1))
     vmem = pl.BlockSpec(memory_space=pltpu.VMEM)
-    return pl.pallas_call(
+    packed = pl.pallas_call(
         functools.partial(reduce_kernel, pairs, lats, piece, scale),
-        out_shape=[
-            jax.ShapeDtypeStruct((taps, ch, hid), F32),
-            jax.ShapeDtypeStruct((taps, hid, hid), F32),
-            jax.ShapeDtypeStruct((taps, ch, hid), F32),
-        ],
+        out_shape=jax.ShapeDtypeStruct((rows, lane), BF),
         in_specs=[vmem] * 6,
-        out_specs=[vmem] * 3,
+        out_specs=vmem,
         scratch_shapes=[
-            pltpu.VMEM((pieces * piece, lane), BF),
-            pltpu.VMEM((pairs * lats * piece, lane), BF),
-            pltpu.VMEM((pairs * lats * piece, lane), BF),
-            pltpu.VMEM((max(pairs - 1, 1), lats * piece, lane), BF),
-            pltpu.VMEM((lats * piece, lane), BF),
-            pltpu.VMEM((max(lats - 1, 1), piece, lane), BF),
-            pltpu.VMEM((pieces * piece, lane), BF),
+            pltpu.VMEM((rows, lane), BF),
+            pltpu.VMEM((segments, pairs * lats * piece, lane), BF),
+            pltpu.VMEM((segments, pairs * lats * piece, lane), BF),
+            pltpu.VMEM((segments, max(pairs - 1, 1), lats * piece, lane), BF),
+            pltpu.VMEM((segments, lats * piece, lane), BF),
+            pltpu.VMEM((segments, max(lats - 1, 1), piece, lane), BF),
+            pltpu.VMEM((rows, lane), BF),
             pltpu.SemaphoreType.DMA((copies,)),
             pltpu.SemaphoreType.DMA((copies,)),
         ],
         compiler_params=pltpu.CompilerParams(collective_id=0, has_side_effects=True),
         name="kernel_term_sum",
     )(*late_terms, *early_terms)
+    return pl.pallas_call(
+        unpack_kernel,
+        grid=(taps,),
+        out_shape=[
+            jax.ShapeDtypeStruct((taps, ch, hid), F32),
+            jax.ShapeDtypeStruct((taps, hid, hid), F32),
+            jax.ShapeDtypeStruct((taps, ch, hid), F32),
+        ],
+        in_specs=[pl.BlockSpec((tap_rows, lane), lambda t: (t, 0))],
+        out_specs=[
+            pl.BlockSpec((1, ch, hid), lambda t: (t, 0, 0)),
+            pl.BlockSpec((1, hid, hid), lambda t: (t, 0, 0)),
+            pl.BlockSpec((1, ch, hid), lambda t: (t, 0, 0)),
+        ],
+        name="unpack_terms",
+    )(packed)
 
 
 def body(state_in, new_state, cot_early, cot_late, kernel_first, kernel_mid, kernel_last):
@@ -464,8 +505,8 @@
     shape = jax.ShapeDtypeStruct
     lanes_v, lanes_1, lanes_2 = (rows + 14) * width, (rows + 12) * width, (rows + 8) * width
     saved_shapes = [
-        ((3 * cp, lanes_v), BF), ((hid, lanes_1), BF), ((hid, lanes_2), BF),
-        ((hid, lanes_1), F32), ((hid, lanes_2), F32),
+        ((3 * cp, lanes_v), BF), ((hid, band), BF), ((hid, band), BF),
+        ((hid, lanes_1), BF), ((hid, lanes_2), BF),
     ]
     fwd_scratch = [((3 * hid, lanes_1), BF), ((3 * hid, lanes_2), BF)]
     bwd_scratch = [
@@ -493,7 +534,7 @@
     late_in = to_step(early_out, new_w, 1, False)
     late_out, late_adj, *late_terms = call(
         late_kernel, "late_both", (late_in, late_cot_w, mask, w1, w2, w3, w1b, w2b, w3b),
-        [((cp, band), BF)] + bwd_outs, saved_shapes + fwd_scratch + bwd_scratch,
+        [((cp, band), BF)] + bwd_outs, saved_shapes[:1] + saved_shapes[3:] + fwd_scratch + bwd_scratch,
     )
     early_cot = to_step(late_adj, early_cot_w, -1, True)
     state_adj, *early_terms = call(

time: 180 us -> 167 us (0.928)
  Pallas kernels: 159 us -> 151 us
  local copies, waits for them, and re-layouts: 20.4 us -> 14.8 us
    pallas_call x3, Pallas kernels: 80.6 us -> 72.1 us  [call(): pl.pallas_call(functools.partial(kernel, rows, width), out_shape=[shape(*...]
    pallas_call x0 -> x1, Pallas kernels: none -> 6.21 us  [all_reduce(): pl.pallas_call(unpack_kernel, grid=(taps,), out_shape=[jax.ShapeDtypeStru...]
    pallas_call x1, Pallas kernels: 41.3 us -> 35.4 us  [all_reduce(): pl.pallas_call(functools.partial(reduce_kernel, pairs, lats, piece, scale...]
    unnamed x23 -> x18, local copies, waits for them, and re-layouts: 9.89 us -> 4.2 us
where the time goes in v3:
time: 167 us; the launch traced here: 166 us
  Pallas kernels  151 us (90%)
  local copies, waits for them, and re-layouts  14.8 us (9%)
    pallas_call x3, Pallas kernels, call(): pl.pallas_call(functools.partial(kernel, rows, width), out_shape=[shape(*...  72.1 us
    pallas_call x1, Pallas kernels, all_reduce(): pl.pallas_call(functools.partial(reduce_kernel, pairs, lats, piece, scale...  35.4 us
    pallas_call x2, Pallas kernels, to_step(): pl.pallas_call(functools.partial(step_kernel, rows, width, steps, lats, d...  19.4 us
    pallas_call x1, Pallas kernels, body(): pl.pallas_call(functools.partial(halo_kernel, rows, width, lats), out_sha...  17.5 us
    pallas_call x1, Pallas kernels, all_reduce(): pl.pallas_call(unpack_kernel, grid=(taps,), out_shape=[jax.ShapeDtypeStru...  6.21 us
    unnamed x18, local copies, waits for them, and re-layouts  4.2 us

profile of v3, /device:TPU:0, one launch (start us, length us, event | category | flops | bytes accessed | tf_op | source)
XLA Modules:
  0.0 166.1 jit_solution(45340508232425329)
XLA Ops:
  0.6 0.1 broadcast_bitcast_fusion
  0.7 0.6 copy.42
  1.3 1.1 copy.18
  2.5 0.0 copy-start.2
  2.5 0.0 copy-start.3
  2.5 0.3 pad_bitcast_fusion
  2.8 0.0 copy-start.4
  2.8 0.0 copy-start.5
  2.8 1.0 reshape.71.w1b
  3.9 0.0 copy-start
  3.9 0.1 copy.19
  3.9 0.9 copy.21.w1
  4.8 0.0 copy-done.2
  4.8 0.0 copy-done.3
  4.8 0.0 copy-start.1
  4.8 0.9 copy_bitcast_fusion.2
  5.7 0.0 copy-done.4
  5.7 0.0 copy-done.5
  5.7 0.9 copy_bitcast_fusion
  6.7 0.0 copy-done
  6.7 1.2 copy.22.w2
  7.9 0.0 copy-done.1
  7.9 0.1 fusion
  7.9 0.9 copy.27.w3b
  8.8 0.3 copy.20
  9.1 1.0 reshape.70.w3
  10.1 0.7 copy.23
  10.8 1.2 copy.26.w2b
  12.0 17.5 %halos.1 = (bf16[80,3840]{1,0:T(8,128)(2,1)}, bf16[80,3840]{1,0:T(8,128)(2,1)}, bf16[80,3840]{1,0:T(8,128)(2,1)}, bf16[80,3840]{1,0:T(8,128)(2,1)}) custom-call(bf16[72,2048]{1,0:T(8,128)(2,1)} %get-tuple-element.56.state, bf16[72,2048]{1,0:T(8,128)(2,1)} %get-tuple-element.55.new, bf16[72,2048]{1,0:T(8,128)(2,1)} %get-tuple-element.54.late, ...), custom_call_target="tpu_custom_call" | custom-call | tf_op jit(solution)/shard_map/halos/pallas_call | solution.py:477
  29.6 18.4 %early_forward.1 = (bf16[80,2048]{1,0:T(8,128)(2,1)}, bf16[240,3840]{1,0:T(8,128)(2,1)}, bf16[192,2048]{1,0:T(8,128)(2,1)}, bf16[192,2048]{1,0:T(8,128)(2,1)}, b...) custom-call(bf16[80,3840]{1,0:T(8,128)(2,1)} %get-tuple-element.27.x, f32[1,3840]{1,0:T(1,128)} %bitcast.74, ...), custom_call_target="tpu_custom_call" | custom-call | tf_op jit(solution)/shard_map/early_forward/pallas_call | solution.py:520
  47.9 5.3 %step_state.1.x = bf16[80,3840]{1,0:T(8,128)(2,1)} custom-call(bf16[80,2048]{1,0:T(8,128)(2,1)} %get-tuple-element.28.block, bf16[80,3840]{1,0:T(8,128)(2,1)} %get-tuple-element.29.base), custom_call_target="tpu_custom_call" | custom-call | tf_op jit(solution)/shard_map/step_state/pallas_call | solution.py:491
  53.2 33.4 %late_both.1 = (bf16[80,2048]{1,0:T(8,128)(2,1)}, bf16[80,2048]{1,0:T(8,128)(2,1)}, f32[3,240,192]{2,1,0:T(8,128)}, f32[3,3,192,192]{3,2,1,0:T(8,128)}, f32[3,240,192]{2,1,0:T(8,128)}) custom-call(bf16[80,3840]{1,0:T(8,128)(2,1)} %step_state.1.x, bf16[80,3840]{1,0:T(8,128)(2,1)} %get-tuple-element.30.cot, f32[1,3840]{1,0:T(1,128)} %bitcast.75, ...), custom_call_target="tpu_custom_call" | custom-call | tf_op jit(solution)/shard_map/late_both/pallas_call | solution.py:520
  86.7 1.0 slice_bitcast_fusion.1
  87.6 0.8 copy.35
  88.4 14.1 %step_cotangent.1.cot = bf16[80,3840]{1,0:T(8,128)(2,1)} custom-call(bf16[80,2048]{1,0:T(8,128)(2,1)} %get-tuple-element.32.block, bf16[80,3840]{1,0:T(8,128)(2,1)} %get-tuple-element.33.base), custom_call_target="tpu_custom_call" | custom-call | tf_op jit(solution)/shard_map/step_cotangent/pallas_call | solution.py:491
  102.5 20.3 %early_backward.1 = (bf16[80,2048]{1,0:T(8,128)(2,1)}, f32[3,240,192]{2,1,0:T(8,128)}, f32[3,3,192,192]{3,2,1,0:T(8,128)}, f32[3,240,192]{2,1,0:T(8,128)}) custom-call(bf16[80,3840]{1,0:T(8,128)(2,1)} %step_cotangent.1.cot, f32[1,3840]{1,0:T(1,128)} %bitcast.76, bf16[80,1728]{1,0:T(8,128)(2,1)} %reshape.71.w1b, bf16[192,1728]{1,0:T(8,128)(2,1)} %copy.26.w2b, ...), custom_call_target="tpu_custom_call" | custom-call | tf_op jit(solution)/shard_map/early_backward/pallas_call | solution.py:520
  122.7 1.0 slice_bitcast_fusion
  123.7 0.8 copy.36
  124.5 35.4 %kernel_term_sum.1.packed = bf16[5120,128]{1,0:T(8,128)(2,1)} custom-call(f32[9,80,192]{2,1,0:T(8,128)} %bitcast.62, f32[9,192,192]{2,1,0:T(8,128)} %bitcast.58, f32[9,80,192]{2,1,0:T(8,128)} %bitcast.63, f32[9,80,192]{2,1,0:T(8,128)} %bitcast.64, f32[9,192,192]{2,1,0:T(8,128)} %bitcast.59, f32[9,80,192]{2,1,0:T(8,128)} %bitcast.65), custom_call_target="tpu_custom_call" | custom-call | tf_op jit(solution)/shard_map/kernel_term_sum/pallas_call | solution.py:416
  159.9 6.2 %unpack_terms.1 = (f32[9,72,192]{2,1,0:T(8,128)}, f32[9,192,192]{2,1,0:T(8,128)}, f32[9,72,192]{2,1,0:T(8,128)}) custom-call(bf16[5120,128]{1,0:T(8,128)(2,1)} %kernel_term_sum.1.packed), custom_call_target="tpu_custom_call" | custom-call | tf_op jit(solution)/shard_map/unpack_terms/pallas_call | solution.py:435
  (1 shorter events, 0.0 us)
Async XLA Ops:
  2.5 2.3 %copy-start.2 = (bf16[72,16,128]{2,1,0:T(8,128)(2,1)S(1)}, bf16[72,16,128]{2,1,0:T(8,128)(2,1)}, u32[]{:S(2)}) copy-start(bf16[72,16,128]{2,1,0:T(8,128)(2,1)} %param.8) | copy-start | bytes 884740
  2.5 2.3 %copy-start.3 = (bf16[1,72,16,128]{3,2,1,0:T(8,128)(2,1)S(1)}, bf16[1,72,16,128]{3,2,1,0:T(8,128)(2,1)}, u32[]{:S(2)}) copy-start(bf16[1,72,16,128]{3,2,1,0:T(8,128)(2,1)} %param.7) | copy-start | bytes 884740
  2.8 2.9 %copy-start.4 = (bf16[1,72,16,128]{3,2,1,0:T(8,128)(2,1)S(1)}, bf16[1,72,16,128]{3,2,1,0:T(8,128)(2,1)}, u32[]{:S(2)}) copy-start(bf16[1,72,16,128]{3,2,1,0:T(8,128)(2,1)} %param.9) | copy-start | bytes 884740
  2.8 2.9 %copy-start.5 = (bf16[1,72,16,128]{3,2,1,0:T(8,128)(2,1)S(1)}, bf16[1,72,16,128]{3,2,1,0:T(8,128)(2,1)}, u32[]{:S(2)}) copy-start(bf16[1,72,16,128]{3,2,1,0:T(8,128)(2,1)} %param.10) | copy-start | bytes 884740
  3.9 2.8 %copy-start = (bf16[9,192,192]{2,1,0:T(8,128)(2,1)S(1)}, bf16[9,192,192]{2,1,0:T(8,128)(2,1)}, u32[]{:S(2)}) copy-start(bf16[9,192,192]{2,1,0:T(8,128)(2,1)} %param.12) | copy-start | bytes 1990660
  4.8 3.1 %copy-start.1 = (bf16[9,72,192]{2,1,0:T(8,128)(2,1)S(1)}, bf16[9,72,192]{2,1,0:T(8,128)(2,1)}, u32[]{:S(2)}) copy-start(bf16[9,72,192]{2,1,0:T(8,128)(2,1)} %param.13) | copy-start | bytes 746500

commit v4 on v3

--- a/solution.py
+++ b/solution.py
@@ -169,7 +169,26 @@
     pl.semaphore_wait(barrier, total)
 
 
-def halo_kernel(rows, width, lats, state, new, late, early, state_w, new_w, late_w, early_w, low, high, send, recv):
+def lay_out_weights(kf, km, kl, w1, w2, w3, w1b, w2b, w3b):
+    taps, ch, hid = kf.shape
+    spare = w3.shape[0] - ch
+
+    def tall(kernel):
+        block = [kernel[t].astype(F32) for t in range(taps)]
+        if kernel.shape[1] == ch and spare:
+            block = [jnp.concatenate([b, jnp.zeros((spare, hid), F32)], axis=0) for b in block]
+        return block
+
+    first, mid, last = tall(kf), tall(km), tall(kl)
+    for block, across, along in ((first, w1, w1b), (mid, w2, w2b), (last, w3b, w3)):
+        across[...] = jnp.transpose(jnp.concatenate(block, axis=0)).astype(BF)
+        along[...] = jnp.concatenate(block, axis=1).astype(BF)
+
+
+def halo_kernel(
+    rows, width, lats, state, new, late, early, kf, km, kl, state_w, new_w, late_w, early_w,
+    w1, w2, w3, w1b, w2b, w3b, low, high, send, recv,
+):
     lat = lax.axis_index("lat")
     step = lax.axis_index("step")
     band, edge = rows * width, HALO * width
@@ -198,6 +217,7 @@
         wide[:ch, :edge] = jnp.zeros((ch, edge), BF)
         wide[:ch, edge + band :] = jnp.zeros((ch, edge), BF)
         wide[ch:, :] = jnp.zeros((wide.shape[0] - ch, band + 2 * edge), BF)
+    lay_out_weights(kf, km, kl, w1, w2, w3, w1b, w2b, w3b)
     for n, (block, wide) in enumerate(blocks):
         @pl.when(guarded(n, has_low))
         def _(n=n, wide=wide):
@@ -458,34 +478,31 @@
     band, edge = rows * width, HALO * width
     lat = lax.axis_index("lat")
 
-    grid_first = jnp.pad(kernel_first.reshape(3, 3, ch, hid), ((0, 0), (0, 0), (0, cp - ch), (0, 0)))
-    grid_last = jnp.pad(kernel_last.reshape(3, 3, ch, hid), ((0, 0), (0, 0), (0, cp - ch), (0, 0)))
-    grid_mid = kernel_mid.reshape(3, 3, hid, hid)
-    w1 = grid_first.transpose(3, 0, 1, 2).reshape(hid, 9 * cp)
-    w2 = grid_mid.transpose(3, 0, 1, 2).reshape(hid, 9 * hid)
-    w3 = grid_last.transpose(2, 0, 1, 3).reshape(cp, 9 * hid)
-    w1b = grid_first.transpose(2, 0, 1, 3).reshape(cp, 9 * hid)
-    w2b = grid_mid.transpose(2, 0, 1, 3).reshape(hid, 9 * hid)
-    w3b = grid_last.transpose(3, 0, 1, 2).reshape(hid, 9 * cp)
-
     ext_row = lat * rows + jnp.arange(rows + 2 * HALO, dtype=jnp.int32) - HALO
     inside = (ext_row >= 0) & (ext_row < rows * lats)
     mask = jnp.repeat(inside.astype(F32), width)[None]
 
     vmem_spec = pl.BlockSpec(memory_space=pltpu.VMEM)
     wide_shape = jax.ShapeDtypeStruct((cp, band + 2 * edge), BF)
-    state_w, new_w, late_cot_w, early_cot_w = pl.pallas_call(
+    weight_shapes = [
+        jax.ShapeDtypeStruct(dims, BF)
+        for dims in ((hid, 9 * cp), (hid, 9 * hid), (cp, 9 * hid), (cp, 9 * hid), (hid, 9 * hid), (hid, 9 * cp))
+    ]
+    state_w, new_w, late_cot_w, early_cot_w, w1, w2, w3, w1b, w2b, w3b = pl.pallas_call(
         functools.partial(halo_kernel, rows, width, lats),
-        out_shape=[wide_shape] * 4,
-        in_specs=[vmem_spec] * 4,
-        out_specs=[vmem_spec] * 4,
+        out_shape=[wide_shape] * 4 + weight_shapes,
+        in_specs=[vmem_spec] * 7,
+        out_specs=[vmem_spec] * 10,
         scratch_shapes=[
             pltpu.VMEM((4, ch, edge), BF), pltpu.VMEM((4, ch, edge), BF),
             pltpu.SemaphoreType.DMA((8,)), pltpu.SemaphoreType.DMA((8,)),
         ],
         compiler_params=pltpu.CompilerParams(collective_id=1, has_side_effects=True),
         name="halos",
-    )(*(block.reshape(ch, band) for block in (state_in[0], new_state, cot_late[0], cot_early[0])))
+    )(
+        *(block.reshape(ch, band) for block in (state_in[0], new_state, cot_late[0], cot_early[0])),
+        kernel_first, kernel_mid, kernel_last,
+    )
 
     def to_step(block, base, distance, adds):
         return pl.pallas_call(

time: 167 us -> 161 us (0.964)
  local copies, waits for them, and re-layouts: 14.8 us -> 8.14 us
    reshape x8 -> x0, local copies, waits for them, and re-layouts: 8.05 us -> none  [the longest x1 1.2 us: body(): w2 = grid_mid.transpose(3, 0, 1, 2).reshape(hid, 9 * hid)]
    unnamed x18 -> x6, local copies, waits for them, and re-layouts: 4.2 us -> 4.18 us
where the time goes in v4:
time: 161 us
  Pallas kernels  152 us (94%)
  local copies, waits for them, and re-layouts  8.14 us (5%)
    pallas_call x3, Pallas kernels, call(): pl.pallas_call(functools.partial(kernel, rows, width), out_shape=[shape(*...  72.1 us
    pallas_call x1, Pallas kernels, all_reduce(): pl.pallas_call(functools.partial(reduce_kernel, pairs, lats, piece, scale...  35.4 us
    pallas_call x2, Pallas kernels, to_step(): pl.pallas_call(functools.partial(step_kernel, rows, width, steps, lats, d...  19.2 us
    pallas_call x1, Pallas kernels, body(): pl.pallas_call(functools.partial(halo_kernel, rows, width, lats), out_sha...  18.9 us
    pallas_call x1, Pallas kernels, all_reduce(): pl.pallas_call(unpack_kernel, grid=(taps,), out_shape=[jax.ShapeDtypeStru...  6.21 us
    unnamed x6, local copies, waits for them, and re-layouts  4.18 us

profile of v4, /device:TPU:0, one launch (start us, length us, event | category | flops | bytes accessed | tf_op | source)
XLA Modules:
  0.0 160.5 jit_solution(7331785627273935729)
XLA Ops:
  0.6 0.1 broadcast_bitcast_fusion
  0.7 0.6 copy.24
  1.3 2.0 %copy_bitcast_fusion.2 = (bf16[72,2048]{1,0:T(8,128)(2,1)}, bf16[72,2048]{1,0:T(8,128)(2,1)}) fusion(bf16[9,8,16,128]{3,2,1,0:T(8,128)(2,1)} %bitcast.43, bf16[9,8,16,128]{3,2,1,0:T(8,128)(2,1)} %bitcast.44), kind=kLoop, calls=%fused_computation.2 | loop fusion | bytes 1179648 | tf_op jit(solution)/shard_map/reshape | solution.py:503
  3.3 2.0 %copy_bitcast_fusion = (bf16[72,2048]{1,0:T(8,128)(2,1)}, bf16[72,2048]{1,0:T(8,128)(2,1)}) fusion(bf16[9,8,16,128]{3,2,1,0:T(8,128)(2,1)} %bitcast.45, bf16[9,8,16,128]{3,2,1,0:T(8,128)(2,1)} %bitcast.46), kind=kLoop, calls=%fused_computation | loop fusion | bytes 1179648 | tf_op jit(solution)/shard_map/reshape;squeeze | solution.py:503
  5.3 18.9 %halos.1 = (bf16[80,3840]{1,0:T(8,128)(2,1)}, bf16[80,3840]{1,0:T(8,128)(2,1)}, bf16[80,3840]{1,0:T(8,128)(2,1)}, bf16[80,3840]{1,0:T(8,128)(2,1)}, bf16[192,720...) custom-call(bf16[72,2048]{1,0:T(8,128)(2,1)} %get-tuple-element.64.s, ...), custom_call_target="tpu_custom_call" | custom-call | tf_op jit(solution)/shard_map/halos/pallas_call | solution.py:491
  24.2 18.3 %early_forward.1 = (bf16[80,2048]{1,0:T(8,128)(2,1)}, bf16[240,3840]{1,0:T(8,128)(2,1)}, bf16[192,2048]{1,0:T(8,128)(2,1)}, bf16[192,2048]{1,0:T(8,128)(2,1)}, b...) custom-call(bf16[80,3840]{1,0:T(8,128)(2,1)} %get-tuple-element.33.x, f32[1,3840]{1,0:T(1,128)} %bitcast.47, ...), custom_call_target="tpu_custom_call" | custom-call | tf_op jit(solution)/shard_map/early_forward/pallas_call | solution.py:537
  42.5 5.3 %step_state.1.x = bf16[80,3840]{1,0:T(8,128)(2,1)} custom-call(bf16[80,2048]{1,0:T(8,128)(2,1)} %get-tuple-element.37.block, bf16[80,3840]{1,0:T(8,128)(2,1)} %get-tuple-element.38.base), custom_call_target="tpu_custom_call" | custom-call | tf_op jit(solution)/shard_map/step_state/pallas_call | solution.py:508
  47.8 33.4 %late_both.1 = (bf16[80,2048]{1,0:T(8,128)(2,1)}, bf16[80,2048]{1,0:T(8,128)(2,1)}, f32[3,240,192]{2,1,0:T(8,128)}, f32[3,3,192,192]{3,2,1,0:T(8,128)}, f32[3,240,192]{2,1,0:T(8,128)}) custom-call(bf16[80,3840]{1,0:T(8,128)(2,1)} %step_state.1.x, bf16[80,3840]{1,0:T(8,128)(2,1)} %get-tuple-element.39.cot, f32[1,3840]{1,0:T(1,128)} %bitcast.48, ...), custom_call_target="tpu_custom_call" | custom-call | tf_op jit(solution)/shard_map/late_both/pallas_call | solution.py:537
  81.2 1.0 slice_bitcast_fusion.1
  82.2 0.8 copy.17
  83.0 13.9 %step_cotangent.1.cot = bf16[80,3840]{1,0:T(8,128)(2,1)} custom-call(bf16[80,2048]{1,0:T(8,128)(2,1)} %get-tuple-element.44.block, bf16[80,3840]{1,0:T(8,128)(2,1)} %get-tuple-element.45.base), custom_call_target="tpu_custom_call" | custom-call | tf_op jit(solution)/shard_map/step_cotangent/pallas_call | solution.py:508
  96.9 20.3 %early_backward.1 = (bf16[80,2048]{1,0:T(8,128)(2,1)}, f32[3,240,192]{2,1,0:T(8,128)}, f32[3,3,192,192]{3,2,1,0:T(8,128)}, f32[3,240,192]{2,1,0:T(8,128)}) custom-call(bf16[80,3840]{1,0:T(8,128)(2,1)} %step_cotangent.1.cot, f32[1,3840]{1,0:T(1,128)} %bitcast.49, bf16[80,1728]{1,0:T(8,128)(2,1)} %get-tuple-element.40.w1b, ...), custom_call_target="tpu_custom_call" | custom-call | tf_op jit(solution)/shard_map/early_backward/pallas_call | solution.py:537
  117.2 1.0 slice_bitcast_fusion
  118.2 0.8 copy.18
  119.0 35.4 %kernel_term_sum.1.packed = bf16[5120,128]{1,0:T(8,128)(2,1)} custom-call(f32[9,80,192]{2,1,0:T(8,128)} %bitcast.37, f32[9,192,192]{2,1,0:T(8,128)} %bitcast.35, f32[9,80,192]{2,1,0:T(8,128)} %bitcast.38, f32[9,80,192]{2,1,0:T(8,128)} %bitcast.39, f32[9,192,192]{2,1,0:T(8,128)} %bitcast.36, f32[9,80,192]{2,1,0:T(8,128)} %bitcast.40), custom_call_target="tpu_custom_call" | custom-call | tf_op jit(solution)/shard_map/kernel_term_sum/pallas_call | solution.py:436
  154.3 6.2 %unpack_terms.1 = (f32[9,72,192]{2,1,0:T(8,128)}, f32[9,192,192]{2,1,0:T(8,128)}, f32[9,72,192]{2,1,0:T(8,128)}) custom-call(bf16[5120,128]{1,0:T(8,128)(2,1)} %kernel_term_sum.1.packed), custom_call_target="tpu_custom_call" | custom-call | tf_op jit(solution)/shard_map/unpack_terms/pallas_call | solution.py:455
  (1 shorter events, 0.0 us)
